TPU v7x, 128 devices: a whole 4x4x4 slice. The times are simulated.
128 devices in a mesh: ctx: 8 (over x, z_hi), frame: 16 (over z_lo, y, core).
Axes of the slice: x: 4, y: 4, z: 4 (z_hi: 2, z_lo: 2; z = z_hi * 2 + z_lo), core: 2. Of those that a mesh axis runs over, the one named last changes fastest.
Arguments:
- queries: bfloat16 [4096, 4096], P('ctx', 'frame'), may hold values from -160 to 160
- keys: bfloat16 [8192, 4096], P('ctx', 'frame'), may hold values from -4 to 4
- values: bfloat16 [8192, 4096], P('ctx', 'frame'), may hold values from -6 to 6
- query_frames: int32 [256], P('ctx'), may hold values from 0 to 383, as said below
- frame_counts: int32 [512], replicated, may hold values from 0 to 16, as said below
- clip_of_frame: int32 [256], P('ctx'), may hold values from 0 to 15, as said below
- in_proj: bfloat16 [4096, 1024], P('frame'), may hold values from -0.09375 to 0.09375
- mlp_up: bfloat16 [1024, 4096], replicated, may hold values from -0.1875 to 0.1875
- mlp_down: bfloat16 [4096, 1024], replicated, may hold values from -0.09375 to 0.09375
- reward_head: float32 [1024], replicated, may hold values from -0.1875 to 0.1875
Outputs:
- query_grad: float32 [4096, 4096], P('ctx', 'frame')
- key_grad: float32 [8192, 4096], P('ctx', 'frame')
- value_grad: float32 [8192, 4096], P('ctx', 'frame')
- clip_reward: float32 [128], P(('ctx', 'frame'))
Inputs may be any that keep to these rules, and one draw needn't show every extreme that they name: `query_frames`: the query patch rows are distinct rows of the first 512 * 3 // 4 patch rows of the video, in increasing order, all of them live; the first and the last of those rows are always among them. `frame_counts`: the live tokens are a prefix of the sequence of at least three quarters of it: rows before the prefix's end are full, one row may be partly live, the rows after it have none, and the last row has none. `clip_of_frame`: within each aligned block of 32 patch row slots every clip number appears exactly 2 times.
All inputs are finite; a program needn't handle non-finite values.
Results may differ from a plain program's by a relative error of at most 0.02.
Values may be sent and summed in bfloat16 or wider, within the bound.
No kernel may reach another device: no remote copies, remote signals or barrier semaphores. Data moves between devices by JAX's collectives and lax.ppermute only.
A program may use at most 192 MiB of HBM per device.

v0:
```python
import functools
import math

import jax
import jax.numpy as jnp
from jax import lax
from jax.experimental import pallas as pl
from jax.experimental.pallas import tpu as pltpu
from jax.sharding import PartitionSpec as P

HD = 128
FTOK = 16
CLIP = 2
EPSILON = 1e-05
SCALE = 1.0 / math.sqrt(HD)
EXP2_SCALE = SCALE * math.log2(math.e)
DEAD = -1e30
EXTRA = 16
CHUNK = 512


f32 = jnp.float32
bf16 = jnp.bfloat16

NN = (((1,), (0,)), ((), ()))
NT = (((1,), (1,)), ((), ()))
TN = (((0,), (0,)), ((), ()))

VMEM = pl.BlockSpec(memory_space=pltpu.VMEM)
SMEM = pl.BlockSpec(memory_space=pltpu.SMEM)


def dot(left, right, dims):
    return lax.dot_general(left, right, dims, preferred_element_type=f32)


def call(kernel, in_specs, outs, scratch=(), work=0):
    return pl.pallas_call(
        kernel,
        cost_estimate=pl.CostEstimate(flops=work, transcendentals=0, bytes_accessed=1 << 20),
        out_shape=[jax.ShapeDtypeStruct(shape, dtype) for shape, dtype in outs],
        in_specs=in_specs,
        out_specs=[VMEM] * len(outs),
        scratch_shapes=list(scratch),
        compiler_params=pltpu.CompilerParams(vmem_limit_bytes=24 * 1024 * 1024),
    )


def split3(x):
    high = x.astype(bf16).astype(f32)
    rest = x - high
    middle = rest.astype(bf16).astype(f32)
    low = (rest - middle).astype(bf16).astype(f32)
    return high, middle, low


def angles(frame):
    lane = lax.broadcasted_iota(jnp.int32, (1, HD), 1).astype(f32)
    half_width = HD // 2
    lane = jnp.where(lane < half_width, lane, lane - half_width)
    angle = frame * jnp.exp(lane * (-math.log(10000.0) / half_width))
    return jnp.cos(angle), jnp.sin(angle)


def spread_angles(table):
    slots = table.shape[1] - FTOK
    cf, sf = table[0, :slots, :], table[1, :slots, :]
    ct, st = table[0, slots:, :], table[1, slots:, :]
    c = cf[:, None, :] * ct[None] - sf[:, None, :] * st[None]
    s = sf[:, None, :] * ct[None] + cf[:, None, :] * st[None]
    rows = slots * FTOK
    lane = lax.broadcasted_iota(jnp.int32, (rows, HD), 1)
    return c.reshape(rows, HD), jnp.where(lane < HD // 2, -1.0, 1.0) * s.reshape(rows, HD)


def fill_table(table, frames):
    slots = table.shape[1] - FTOK
    table[0, :slots, :], table[1, :slots, :] = angles(frames * FTOK)
    token = lax.broadcasted_iota(jnp.int32, (FTOK, HD), 0).astype(f32)
    table[0, slots:, :], table[1, slots:, :] = angles(token)


def rotate_query_kernel(ctx, frames, x, own, other, table, places):
    slots = frames.shape[0]
    for i in range(slots):
        places[i : i + 1, :] = jnp.full((1, HD), frames[i].astype(f32))
    fill_table(table, places[...])
    c, s = spread_angles(table)
    for which in range(2):

        @pl.when(ctx[0] % 2 == which)
        def _():
            for side, out in ((which, own), (1 - which, other)):
                head = x[:, side * HD : side * HD + HD].astype(f32)
                turned = head * c + pltpu.roll(head, HD // 2, 1) * s
                out[...] = turned.T.astype(bf16)


def rotate_key_kernel(ctx, x, v, own, other, table):
    slots = x.shape[0] // FTOK
    row = lax.broadcasted_iota(jnp.int32, (slots, HD), 0)
    fill_table(table, (row + ctx[0] * slots).astype(f32))
    c, s = spread_angles(table)
    for which in range(2):

        @pl.when(ctx[0] % 2 == which)
        def _():
            for side, out in ((which, own), (1 - which, other)):
                cols = slice(side * HD, side * HD + HD)
                head = x[:, cols].astype(f32)
                turned = head * c + pltpu.roll(head, HD // 2, 1) * s
                out[:, :HD] = turned.astype(bf16)
                out[:, HD:] = v[:, cols]


def fill_keys(ctx, counts, starts, kv_refs, kaug):
    rows = kv_refs[0].shape[0]
    lane = lax.broadcasted_iota(jnp.int32, (rows, HD), 1)
    row = lax.broadcasted_iota(jnp.int32, (rows, HD), 0)
    ones = jnp.where((lane >= 3) & (lane < 6), 1.0, 0.0)
    live = jnp.sum(jnp.sum(counts[...].astype(f32), axis=0, keepdims=True), axis=1, keepdims=True)
    me = ctx[0]
    owners = (me, me ^ 1, 6 - me + 2 * (me % 2), 7 - me)
    for part, ref in enumerate(kv_refs):
        place = (row + owners[starts[part]] * rows).astype(f32)
        bias = jnp.where(place < live, 0.0, DEAD)
        kaug[part * rows : part * rows + rows, :HD] = ref[:, :HD]
        kaug[part * rows : part * rows + rows, HD:] = jnp.where(lane == 6, bias, ones).astype(bf16)


def forward_kernel(ctx, counts, *refs, blocks, starts, first):
    refs = list(refs)

    def take(count):
        taken = refs[:count]
        del refs[:count]
        return taken

    pieces = len(starts)
    q_refs = take(blocks)
    kv_refs = take(pieces)
    if not first:
        acc_in, stat_in = take(2)
    if first:
        acc_out, stat_out = take(2)
    else:
        out_refs = take(blocks)
    kaug, v_t, q_all, *scores = take(5)
    if not first:
        (out_all,) = take(1)
    rows = kv_refs[0].shape[0]
    keys = pieces * rows
    wide = q_refs[0].shape[1]
    fill_keys(ctx, counts, starts, kv_refs, kaug)
    for part, ref in enumerate(kv_refs):
        v_t[:, part * rows : part * rows + rows] = ref[:, HD:].astype(f32).T.astype(bf16)
    sub = lax.broadcasted_iota(jnp.int32, (HD, wide), 0)
    tail = jnp.where(sub == 6, 1.0, 0.0).astype(bf16)
    for i in range(blocks):
        q_all[i, :HD, :] = q_refs[i][...]
        q_all[i, HD:, :] = tail
    spans = [slice(j * CHUNK, j * CHUNK + CHUNK) for j in range(keys // CHUNK)]

    def score(i, slot, span, top):
        s = dot(kaug[span, :], q_all[i], NN)
        scores[slot][span, :] = s
        return jnp.maximum(top, jnp.max(s, axis=0, keepdims=True))

    def start(i):
        return jnp.full((1, wide), -jnp.inf, f32) if first else stat_in[i, 0:1, :]

    def block(i, slot, top, follow):
        if first:
            total = jnp.zeros((1, wide), f32)
            acc = jnp.zeros((HD, wide), f32)
        else:
            shrink = jnp.exp2((stat_in[i, 0:1, :] - top) * EXP2_SCALE)
            total = stat_in[i, 1:2, :] * shrink
            acc = acc_in[i] * shrink
        following = start(follow)
        for span in spans:
            following = score(follow, 1 - slot, span, following)
            p = jnp.exp2((scores[slot][span, :] - top) * EXP2_SCALE)
            total = total + jnp.sum(p, axis=0, keepdims=True)
            acc = acc + dot(v_t[:, span], p.astype(bf16), NN)
        if first:
            acc_out[i] = acc
            which = lax.broadcasted_iota(jnp.int32, (8, wide), 0)
            stat_out[i] = jnp.where(which == 0, top, total)
        else:
            out_all[i, :HD, :] = (acc / total).astype(bf16)
            high, middle, low = split3(top + jnp.log(total) * (1.0 / SCALE))
            which = lax.broadcasted_iota(jnp.int32, (EXTRA, wide), 0)
            rest = jnp.where(which == 1, middle, jnp.where(which == 2, low, 0.0))
            out_all[i, HD:, :] = jnp.where(which == 0, high, rest).astype(bf16)
        return following

    top = start(0)
    for span in spans:
        top = score(0, 0, span, top)

    def pair(t, top):
        middle = block(2 * t, 0, top, 2 * t + 1)
        return block(2 * t + 1, 1, middle, jnp.minimum(2 * t + 2, blocks - 1))

    lax.fori_loop(0, blocks // 2, pair, top)
    if not first:
        for i in range(blocks):
            out_refs[i][...] = out_all[i]


def forward(ctx, counts, q_blocks, kv_pieces, starts, before=None):
    blocks = len(q_blocks)
    wide = q_blocks[0].shape[1]
    keys = len(kv_pieces) * kv_pieces[0].shape[0]
    first = before is None
    if first:
        outs = [((blocks, HD, wide), f32), ((blocks, 8, wide), f32)]
    else:
        outs = [((HD + EXTRA, wide), bf16)] * blocks
    args = [*q_blocks, *kv_pieces] + ([] if first else list(before))
    return call(
        functools.partial(forward_kernel, blocks=blocks, starts=starts, first=first),
        [SMEM] + [VMEM] * (len(args) + 1),
        outs,
        [
            pltpu.VMEM((keys, 2 * HD), bf16),
            pltpu.VMEM((HD, keys), bf16),
            pltpu.VMEM((blocks, 2 * HD, wide), bf16),
            pltpu.VMEM((keys, wide), f32),
            pltpu.VMEM((keys, wide), f32),
        ]
        + ([] if first else [pltpu.VMEM((blocks, HD + EXTRA, wide), bf16)]),
        work=10**10,
    )(ctx, counts, *args)


def one_hot(place):
    rows = place.shape[1]
    row = lax.broadcasted_iota(jnp.int32, (rows, rows), 0)
    return jnp.where(row == place[...], 1.0, 0.0).astype(bf16)


def combine_kernel(ctx, place, *refs):
    partial, (out_t, logs, c0, c1, c2, c3) = refs[:4], refs[4:]
    wide = partial[0].shape[1]
    for side in range(2):
        sums = []
        for ref in partial[2 * side : 2 * side + 2]:
            tail = ref[HD:, :].astype(f32)
            sums.append(tail[0:1] + tail[1:2] + tail[2:3])
        top = functools.reduce(jnp.maximum, sums)
        weight = [jnp.exp2((s - top) * EXP2_SCALE) for s in sums]
        total = sum(weight)
        acc = jnp.zeros((HD, wide), f32)
        for w, ref in zip(weight, partial[2 * side : 2 * side + 2]):
            acc = acc + (w / total) * ref[:HD, :].astype(f32)
        logs[side, :, :] = jnp.broadcast_to(top + jnp.log(total) * (1.0 / SCALE), (8, wide))
        head = ctx[0] % 2 if side == 0 else 1 - ctx[0] % 2
        out_t[pl.ds(pl.multiple_of(head * HD, HD), HD), :] = acc.astype(bf16)
    grouped = dot(one_hot(place), out_t[...], NT).astype(bf16)
    quarter = wide // 4
    for i, ref in enumerate((c0, c1, c2, c3)):
        ref[...] = grouped[i * quarter : i * quarter + quarter]


def project_kernel(o0, o1, o2, o3, w0, w1, w2, w3, x0, x1, x2, x3):
    total = None
    for o, w in ((o0, w0), (o1, w1), (o2, w2), (o3, w3)):
        term = dot(o[...], w[...], NN)
        total = term if total is None else total + term
    rows = x0.shape[0]
    for i, ref in enumerate((x0, x1, x2, x3)):
        ref[...] = total[i * rows : i * rows + rows].astype(ref.dtype)


def unproject_kernel(g0, g1, g2, g3, w0, w1, w2, w3, d0, d1, d2, d3, g):
    rows = g0.shape[0]
    for i, ref in enumerate((g0, g1, g2, g3)):
        g[i * rows : i * rows + rows, :] = ref[...]
    for w, d in ((w0, d0), (w1, d1), (w2, d2), (w3, d3)):
        d[...] = dot(g[...], w[...], NT).astype(bf16)


def center(x):
    mean = jnp.mean(x, axis=1, keepdims=True)
    shifted = x - mean
    rate = lax.rsqrt(jnp.mean(shifted * shifted, axis=1, keepdims=True) + EPSILON)
    return shifted * rate, rate


def center_grad(grad, normed, rate):
    return rate * (
        grad
        - jnp.mean(grad, axis=1, keepdims=True)
        - normed * jnp.mean(grad * normed, axis=1, keepdims=True)
    )


def reward_kernel(counts, x0, x1, x2, x3, head, up, down, grad_out, reward_out, slopes):
    steps, _, part = slopes.shape
    vision = up.shape[0]

    def piece(j):
        return pl.ds(pl.multiple_of(j * part, part), part)

    rows = x0.shape[0]

    def live(shape, axis):
        row = lax.broadcasted_iota(jnp.int32, shape, axis)
        left = jnp.where(row < FTOK, counts[0], counts[1] + FTOK)
        return jnp.where(row < left, 1.0, 0.0)

    x = x0[...].astype(f32) + x1[...].astype(f32) + x2[...].astype(f32) + x3[...].astype(f32)
    normed, rate = center(x)
    low_normed = normed.astype(bf16)
    c0 = math.sqrt(2.0 / math.pi)
    c1 = 0.044715

    def upward(j, hidden):
        before = dot(low_normed, up[:, piece(j)], NN)
        square = before * before
        tanh = jnp.tanh(c0 * before * (1.0 + c1 * square))
        half = 0.5 * (1.0 + tanh)
        slope = half + 0.5 * before * (1.0 - tanh * tanh) * (c0 * (1.0 + 3.0 * c1 * square))
        slopes[j] = slope
        return hidden + dot((before * half).astype(bf16), down[piece(j), :], NN)

    hidden = lax.fori_loop(0, steps, upward, jnp.zeros((rows, vision), f32))
    alive = live((rows, 1), 0)
    count = jnp.sum(alive, axis=0, keepdims=True)
    pooled = jnp.sum(hidden * alive, axis=0, keepdims=True) / count
    pooled_normed, pooled_rate = center(pooled)
    reward = count * jnp.sum(pooled_normed * head[...], axis=1, keepdims=True)
    reward_out[...] = jnp.broadcast_to(reward, reward_out.shape)
    pooled_grad = center_grad(count * head[...], pooled_normed, pooled_rate) / count
    high, middle, low = split3(pooled_grad)
    which = lax.broadcasted_iota(jnp.int32, (EXTRA, vision), 0)
    pieces = jnp.where(which == 0, high, jnp.where(which == 1, middle, jnp.where(which == 2, low, 0.0)))
    pieces_b = pieces.astype(bf16)
    alive_t = live((1, rows), 1)

    def downward(j, normed_grad):
        spread = jnp.sum(dot(pieces_b, down[piece(j), :], NT), axis=0, keepdims=True)
        before_grad = (spread * slopes[j] * alive).astype(bf16)
        return normed_grad + dot(before_grad, up[:, piece(j)], NT)

    normed_grad = lax.fori_loop(0, steps, downward, jnp.zeros((rows, vision), f32))
    grad_out[...] = center_grad(normed_grad, normed, rate).astype(bf16)


def reward_call(counts, inputs, head, mlp_up, mlp_down):
    vision, hidden = mlp_up.shape
    steps = 8
    part = hidden // steps
    rows = inputs[0].shape[0]
    return call(
        reward_kernel,
        [SMEM] + [VMEM] * 7,
        [((rows, vision), bf16), ((8, HD), f32)],
        [
            pltpu.VMEM((steps, rows, part), f32),
        ],
    )(counts, *inputs, head.reshape(1, -1), mlp_up, mlp_down)


def ungroup_kernel(ctx, place, d0, d1, d2, d3, out_t, logs, ps, po, grad):
    quarter = d0.shape[0]
    for i, ref in enumerate((d0, d1, d2, d3)):
        grad[i * quarter : i * quarter + quarter, :] = ref[...]
    wide = place.shape[1]
    grad_t = dot(grad[...], one_hot(place), TN)
    product = grad_t * out_t[...].astype(f32)
    which = lax.broadcasted_iota(jnp.int32, (EXTRA, wide), 0)
    for head in range(2):
        delta = jnp.sum(product[head * HD : head * HD + HD], axis=0, keepdims=True)
        for side, ref in enumerate((ps, po)):

            @pl.when(head == (ctx[0] % 2 if side == 0 else 1 - ctx[0] % 2))
            def _():
                ref[:HD, :] = grad_t[head * HD : head * HD + HD].astype(bf16)
                rows = split3(delta) + split3(-logs[side, 0:1, :])
                tail = jnp.where(which == 6, 1.0, 0.0)
                for i, piece in enumerate(rows):
                    tail = jnp.where(which == i, piece, tail)
                ref[HD:, :] = tail.astype(bf16)


def backward_kernel(ctx, counts, *refs, blocks, starts, first, last):
    refs = list(refs)

    def take(count):
        taken = refs[:count]
        del refs[:count]
        return taken

    pieces = len(starts)
    q_refs = take(blocks)
    g_refs = take(blocks)
    kv_refs = take(pieces)
    if not first:
        (dq_in,) = take(1)
    dq_refs = take(blocks) if last else take(1)
    out_refs = take(pieces + 1) if last else take(pieces)
    kaug, vaug, k_t, q_all, g_all, dk, dv = take(7)
    if last:
        (dq_all,) = take(1)
    rows = kv_refs[0].shape[0]
    keys = pieces * rows
    wide = q_refs[0].shape[1]
    fill_keys(ctx, counts, starts, kv_refs, kaug)
    lane = lax.broadcasted_iota(jnp.int32, (rows, HD), 1)
    minus = jnp.where(lane < 3, -1.0, 0.0).astype(bf16)
    for part, ref in enumerate(kv_refs):
        where = slice(part * rows, part * rows + rows)
        vaug[where, :HD] = ref[:, HD:]
        vaug[where, HD:] = minus
        k_t[:, where] = ref[:, :HD].astype(f32).T.astype(bf16)
    dk[...] = jnp.zeros_like(dk)
    dv[...] = jnp.zeros_like(dv)
    blank = jnp.zeros((HD - EXTRA, wide), bf16)
    for i in range(blocks):
        q_all[i, :HD, :] = q_refs[i][...]
        q_all[i, HD : HD + EXTRA, :] = g_refs[i][HD:, :]
        q_all[i, HD + EXTRA :, :] = blank
        g_all[i, : HD + EXTRA, :] = g_refs[i][...]
        g_all[i, HD + EXTRA :, :] = blank

    def block(i, carry):
        query = q_all[i]
        grad = g_all[i]
        acc = jnp.zeros((HD, wide), f32) if first else dq_in[i]
        for j in range(keys // CHUNK):
            part = slice(j * CHUNK, j * CHUNK + CHUNK)
            p = jnp.exp2(dot(kaug[part, :], query, NN) * EXP2_SCALE)
            ds = (p * dot(vaug[part, :], grad, NN)).astype(bf16)
            dv[part, :] += dot(p.astype(bf16), grad[:HD], NT)
            dk[part, :] += dot(ds, query[:HD], NT)
            acc = acc + dot(k_t[:, part], ds, NN)
        if last:
            dq_all[i] = (acc * SCALE).astype(bf16)
        else:
            dq_refs[0][i] = acc
        return carry

    lax.fori_loop(0, blocks, block, 0)
    if last:
        for i in range(blocks):
            dq_refs[i][...] = dq_all[i]
    for part in range(pieces):
        where = slice(part * rows, part * rows + rows)
        if last and part == 0:
            out_refs[0][...] = dk[where, :] * SCALE
            out_refs[1][...] = dv[where, :]
        else:
            ref = out_refs[part + 1 if last else part]
            ref[:, :HD] = (dk[where, :] * SCALE).astype(bf16)
            ref[:, HD:] = dv[where, :].astype(bf16)


def backward(ctx, counts, q_blocks, g_blocks, kv_pieces, starts, before=None):
    blocks = len(q_blocks)
    pieces = len(kv_pieces)
    wide = q_blocks[0].shape[1]
    rows = kv_pieces[0].shape[0]
    keys = pieces * rows
    last = before is not None
    packed = ((rows, 2 * HD), bf16)
    if last:
        outs = [((HD, wide), bf16)] * blocks + [((rows, HD), f32)] * 2 + [packed] * (pieces - 1)
    else:
        outs = [((blocks, HD, wide), f32)] + [packed] * pieces
    scratch = [
        pltpu.VMEM((keys, 2 * HD), bf16),
        pltpu.VMEM((keys, 2 * HD), bf16),
        pltpu.VMEM((HD, keys), bf16),
        pltpu.VMEM((blocks, 2 * HD, wide), bf16),
        pltpu.VMEM((blocks, 2 * HD, wide), bf16),
        pltpu.VMEM((keys, HD), f32),
        pltpu.VMEM((keys, HD), f32),
    ]
    if last:
        scratch.append(pltpu.VMEM((blocks, HD, wide), bf16))
    args = [*q_blocks, *g_blocks, *kv_pieces] + ([before] if last else [])
    out = call(
        functools.partial(
            backward_kernel, blocks=blocks, starts=starts, first=not last, last=last
        ),
        [SMEM] + [VMEM] * (len(args) + 1),
        outs,
        scratch,
        work=2 * 10**10,
    )(ctx, counts, *args)
    count = blocks if last else 1
    return (out[:blocks] if last else out[0]), out[count:]


def unrotate(x, c, s):
    return x * c - pltpu.roll(x, HD // 2, 1) * s


def query_grad_kernel(ctx, table, d0, d1, d2, d3, out):
    c, s = spread_angles(table)
    for which in range(2):

        @pl.when(ctx[0] % 2 == which)
        def _():
            for head, one, two in ((which, d0, d1), (1 - which, d2, d3)):
                total = one[...].astype(f32) + two[...].astype(f32)
                out[:, head * HD : head * HD + HD] = unrotate(total.T, c, s)


def key_grad_kernel(ctx, table, dk, dv, far, par, far_par, dk_out, dv_out):
    c, s = spread_angles(table)
    for which in range(2):

        @pl.when(ctx[0] % 2 == which)
        def _():
            cols = slice(which * HD, which * HD + HD)
            dk_out[:, cols] = unrotate(dk[...] + far[:, :HD].astype(f32), c, s)
            dv_out[:, cols] = dv[...] + far[:, HD:].astype(f32)
            cols = slice(HD - which * HD, 2 * HD - which * HD)
            total = par[...].astype(f32) + far_par[...].astype(f32)
            dk_out[:, cols] = unrotate(total[:, :HD], c, s)
            dv_out[:, cols] = total[:, HD:]


def ctx_swap(turn, flip):
    def target(x, z):
        x = (x, x ^ 1, 3 - x)[turn]
        return x * 2 + (z ^ flip)

    return [(x * 2 + z, target(x, z)) for x in range(4) for z in range(2)]


def send_ctx(array, turn, flip):
    return lax.ppermute(array, "ctx", ctx_swap(turn, flip))


def frame_xor(mask):
    return [(i, i ^ mask) for i in range(16)]


QUAD_MASKS = (0, 1, 8, 9)
Y_MASKS = (0, 2, 4, 6)


def send_frame(array, mask):
    return array if mask == 0 else lax.ppermute(array, "frame", frame_xor(mask))


def exchange(blocks):
    same, near, other, near_other = blocks
    return [same, send_ctx(near, 1, 0), send_ctx(other, 0, 1), send_ctx(near_other, 1, 1)]


def shards(
    queries,
    keys,
    values,
    query_frames,
    frame_counts,
    clip_of_frame,
    in_proj,
    mlp_up,
    mlp_down,
    reward_head,
):
    ctx_index = lax.axis_index("ctx")
    frame_index = lax.axis_index("frame")
    query_rows = queries.shape[0]
    key_rows = keys.shape[0]
    frame_slots = query_frames.shape[0]
    key_frames = frame_counts.shape[0]
    in_frame = jnp.arange(FTOK, dtype=jnp.int32)
    ctx = ctx_index.reshape(1).astype(jnp.int32)
    counts = frame_counts.reshape(-1, HD)
    packed_rows = ((key_rows, 2 * HD), bf16)
    key_table = (2, key_rows // FTOK + FTOK, HD)
    kv_own, kv_send, key_table = call(
        rotate_key_kernel,
        [SMEM] + [VMEM] * 2,
        [packed_rows] * 2 + [(key_table, f32)],
    )(ctx, keys, values)
    kv_far = send_ctx(kv_own, 2, 0)
    qs, qo, query_table = call(
        rotate_query_kernel,
        [SMEM] * 2 + [VMEM],
        [((HD, query_rows), bf16)] * 2 + [((2, frame_slots + FTOK, HD), f32)],
        [pltpu.VMEM((frame_slots, HD), f32)],
    )(ctx, query_frames, queries)
    q_blocks = exchange((qs, qs, qo, qo))
    kv_send, _ = lax.optimization_barrier((kv_send, qs))
    kv_par = send_ctx(kv_send, 0, 1)
    kv_far_par = send_ctx(kv_send, 2, 1)

    slot_index = jnp.arange(frame_slots, dtype=jnp.int32)
    same_clip = clip_of_frame[:, None] == clip_of_frame[None, :]
    earlier = slot_index[None, :] < slot_index[:, None]
    rank = jnp.sum(jnp.logical_and(same_clip, earlier), axis=1).astype(jnp.int32)
    away = clip_of_frame ^ frame_index
    quad = (away >> 3) * 2 + (away & 1)
    slot_place = (quad * 4 + ((away >> 1) & 3)) * CLIP + rank
    place = (slot_place[:, None] * FTOK + in_frame[None, :]).reshape(1, query_rows)
    frame_match = query_frames[:, None] == jnp.arange(key_frames, dtype=jnp.int32)[None, :]
    slot_counts = jnp.sum(jnp.where(frame_match, frame_counts[None, :], 0), axis=1)
    mine = slot_place[None, :] == jnp.arange(CLIP, dtype=jnp.int32)[:, None]
    my_counts = jnp.sum(jnp.where(mine, slot_counts[None, :], 0), axis=1).astype(jnp.int32)

    before = forward(ctx, counts, q_blocks, (kv_own, kv_far), (0, 2))
    kv_par, kv_far_par, in_proj, _ = lax.optimization_barrier(
        (kv_par, kv_far_par, in_proj, before[1])
    )
    near = send_frame(in_proj, 8)
    partial = forward(ctx, counts, q_blocks, (kv_par, kv_far_par), (1, 3), before)
    in_proj, near_late, _ = lax.optimization_barrier((in_proj, near, partial[0]))
    weights = (in_proj, send_frame(in_proj, 1), near_late, send_frame(near_late, 1))
    partial = exchange(partial)
    width = queries.shape[1]
    quarter = query_rows // 4
    out_t, logs, *chunks = call(
        combine_kernel,
        [SMEM] + [VMEM] * 5,
        [((width, query_rows), bf16), ((2, 8, query_rows), f32)] + [((quarter, width), bf16)] * 4,
    )(ctx, place, *partial)
    chunks = [send_frame(chunk, mask) for chunk, mask in zip(chunks, QUAD_MASKS)]
    vision = in_proj.shape[1]
    clip_rows = CLIP * FTOK
    inputs = call(
        project_kernel,
        [VMEM] * 8,
        [((clip_rows, vision), f32)] + [((clip_rows, vision), bf16)] * 3,
    )(*chunks, *weights)
    inputs = [send_frame(x, mask) for x, mask in zip(inputs, Y_MASKS)]
    input_grad, reward = reward_call(my_counts, inputs, reward_head, mlp_up, mlp_down)
    grads = [send_frame(input_grad, mask) for mask in Y_MASKS]
    grads = call(
        unproject_kernel,
        [VMEM] * 8,
        [((quarter, width), bf16)] * 4,
        [pltpu.VMEM((quarter, vision), bf16)],
    )(*grads, *weights)
    grads = [send_frame(grad, mask) for grad, mask in zip(grads, QUAD_MASKS)]
    packed = (HD + EXTRA, query_rows)
    gs, go = call(
        ungroup_kernel,
        [SMEM] + [VMEM] * 7,
        [(packed, bf16)] * 2,
        [pltpu.VMEM((query_rows, width), bf16)],
    )(ctx, place, *grads, out_t, logs)
    g_blocks = exchange((gs, gs, go, go))
    dq, (d_par, d_far_par) = backward(ctx, counts, q_blocks, g_blocks, (kv_par, kv_far_par), (1, 3))
    d_par = send_ctx(d_par, 0, 1)
    d_far_par = send_ctx(d_far_par, 2, 1)
    dq, (dk_own, dv_own, d_far) = backward(
        ctx, counts, q_blocks, g_blocks, (kv_own, kv_far), (0, 2), dq
    )
    d_far = send_ctx(d_far, 2, 0)
    dq = exchange(dq)
    (query_grad,) = call(
        query_grad_kernel,
        [SMEM] + [VMEM] * 5,
        [((query_rows, width), f32)],
    )(ctx, query_table, *dq)
    key_grad, value_grad = call(
        key_grad_kernel,
        [SMEM] + [VMEM] * 6,
        [((key_rows, width), f32)] * 2,
    )(ctx, key_table, dk_own, dv_own, d_far, d_par, d_far_par)
    return query_grad, key_grad, value_grad, reward[0, :1]


def solution(mesh):
    return jax.shard_map(
        shards,
        mesh=mesh,
        in_specs=(
            P("ctx", "frame"),
            P("ctx", "frame"),
            P("ctx", "frame"),
            P("ctx"),
            P(),
            P("ctx"),
            P("frame", None),
            P(),
            P(),
            P(),
        ),
        out_specs=(P("ctx", "frame"), P("ctx", "frame"), P("ctx", "frame"), P(("ctx", "frame"))),
        check_vma=False,
    )
```

profile of v0, /device:TPU:0, one launch (start us, length us, event | category | flops | bytes accessed | tf_op | source)
XLA Modules:
  0.0 191.2 jit_solution(15313536676458941403)
XLA Ops:
  3.6 2.9 %collective-permute-start.5 = (bf16[1024,256]{1,0:T(8,128)(2,1)S(1)}, bf16[1024,256]{1,0:T(8,128)(2,1)S(1)}, u32[]{:S(2)}, u32[]{:S(2)}) collective-permute-start(bf16[1024,256]{1,0:T(8,128)(2,1)S(1)} %get-tuple-element.57.refs_4_.refs_8_), channel_id=1, source_target_pairs={{0,96},{16,112},{32,64},{48,80},{64,32},{80,48},{96,0},{112,16},{1... | collective-permute-start | bytes 1572872 | tf_op jit(solution)/shard_map/ppermute | solution.py:537
  9.2 3.6 %collective-permute-start.2 = (bf16[128,512]{1,0:T(8,128)(2,1)S(1)}, bf16[128,512]{1,0:T(8,128)(2,1)S(1)}, u32[]{:S(2)}, u32[]{:S(2)}) collective-permute-start(bf16[128,512]{1,0:T(8,128)(2,1)S(1)} %get-tuple-element.54), channel_id=1, source_target_pairs={{0,48},{16,32},{32,16},{48,0},{64,112},{80,96},{96,80},{112,64},{1... | collective-permute-start | bytes 393224 | tf_op jit(solution)/shard_map/ppermute | solution.py:537
  14.6 3.4 %collective-permute-start.4 = (bf16[1024,256]{1,0:T(8,128)(2,1)S(1)}, bf16[1024,256]{1,0:T(8,128)(2,1)S(1)}, u32[]{:S(2)}, u32[]{:S(2)}) collective-permute-start(bf16[1024,256]{1,0:T(8,128)(2,1)S(1)} %get-tuple-element.56), channel_id=1, source_target_pairs={{0,112},{16,96},{32,80},{48,64},{64,48},{80,32},{96,16},{112,0},{1... | collective-permute-start | bytes 1572872 | tf_op jit(solution)/shard_map/ppermute | solution.py:537
  19.6 2.9 %collective-permute-start.3 = (bf16[1024,256]{1,0:T(8,128)(2,1)S(1)}, bf16[1024,256]{1,0:T(8,128)(2,1)S(1)}, u32[]{:S(2)}, u32[]{:S(2)}) collective-permute-start(bf16[1024,256]{1,0:T(8,128)(2,1)S(1)} %get-tuple-element.56), channel_id=1, source_target_pairs={{0,16},{16,0},{32,48},{48,32},{64,80},{80,64},{96,112},{112,96},{1... | collective-permute-start | bytes 1572872 | tf_op jit(solution)/shard_map/ppermute | solution.py:537
  27.3 6.0 %shard_map.131 = (f32[4,128,512]{2,1,0:T(8,128)S(1)}, f32[4,8,512]{2,1,0:T(8,128)S(1)}) custom-call(s32[1]{0:T(128)} %bitcast.ctx, s32[4,128]{1,0:T(4,128)S(1)} %bitcast.5, bf16[128,512]{1,0:T(8,128)(2,1)S(1)} %get-tuple-element.53.refs_0_, bf16[128,512]{1,0:T(8,128)(2,1)S(1)} %copy-done.29, bf16[128,512]{1,0:T(8,128)(2,1)S(1)} %copy-done.25, ...), custom_call_target="tpu_custom_call" | custom-call | flops 10000000000 | bytes 1048576 | tf_op jit(solution)/shard_map/pallas_call | solution.py:222
  33.3 10.6 %collective-permute-done.3.refs_4_.refs_8_ = bf16[1024,256]{1,0:T(8,128)(2,1)S(1)} collective-permute-done((bf16[1024,256]{1,0:T(8,128)(2,1)S(1)}, bf16[1024,256]{1,0:T(8,128)(2,1)S(1)}, u32[]{:S(2)}, u32[]{:S(2)}) %collective-permute-start.3) | collective-permute-done | bytes 524320 | tf_op jit(solution)/shard_map/ppermute | solution.py:537
  45.9 7.1 %shard_map.132 = (bf16[144,512]{1,0:T(8,128)(2,1)S(1)}, bf16[144,512]{1,0:T(8,128)(2,1)}, bf16[144,512]{1,0:T(8,128)(2,1)}, bf16[144,512]{1,0:T(8,128)(2,1)S(1)}) custom-call(s32[1]{0:T(128)} %bitcast.ctx, s32[4,128]{1,0:T(4,128)S(1)} %bitcast.6, bf16[128,512]{1,0:T(8,128)(2,1)S(1)} %copy-done.18, bf16[128,512]{1,0:T(8,128)(2,1)S(1)} %copy-done.30, ...), custom_call_target="tpu_custom_call" | custom-call | flops 10000000000 | bytes 1048576 | tf_op jit(solution)/shard_map/pallas_call | solution.py:222
  53.0 4.3 %collective-permute-done.12.w2 = bf16[256,1024]{1,0:T(8,128)(2,1)S(1)} collective-permute-done((bf16[256,1024]{1,0:T(8,128)(2,1)S(1)}, bf16[256,1024]{1,0:T(8,128)(2,1)S(1)}, u32[]{:S(2)}, u32[]{:S(2)}) %collective-permute-start.12) | collective-permute-done | bytes 524320 | tf_op jit(solution)/shard_map/ppermute | solution.py:549
  64.3 4.5 %collective-permute-done.7.refs_2_ = bf16[144,512]{1,0:T(8,128)(2,1)S(1)} collective-permute-done((bf16[144,512]{1,0:T(8,128)(2,1)}, bf16[144,512]{1,0:T(8,128)(2,1)S(1)}, u32[]{:S(2)}, u32[]{:S(2)}) %collective-permute-start.7) | collective-permute-done | bytes 147488 | tf_op jit(solution)/shard_map/ppermute | solution.py:537
  71.4 2.9 %collective-permute-done.10.o2 = bf16[128,256]{1,0:T(8,128)(2,1)S(1)} collective-permute-done((bf16[128,256]{1,0:T(8,128)(2,1)S(1)}, bf16[128,256]{1,0:T(8,128)(2,1)S(1)}, u32[]{:S(2)}, u32[]{:S(2)}) %collective-permute-start.10) | collective-permute-done | bytes 65568 | tf_op jit(solution)/shard_map/ppermute | solution.py:549
  77.0 2.9 %collective-permute-start.16 = (bf16[32,1024]{1,0:T(8,128)(2,1)S(1)}, bf16[32,1024]{1,0:T(8,128)(2,1)S(1)}, u32[]{:S(2)}, u32[]{:S(2)}) collective-permute-start(bf16[32,1024]{1,0:T(8,128)(2,1)S(1)} %get-tuple-element.75), channel_id=1, source_target_pairs={{0,4},{1,5},{2,6},{3,7},{4,0},{5,1},{6,2},{7,3},{8,12},{9,13},{10,... | collective-permute-start | bytes 196616 | tf_op jit(solution)/shard_map/ppermute | solution.py:549
  80.2 3.3 %collective-permute-done.16.x2 = bf16[32,1024]{1,0:T(8,128)(2,1)S(1)} collective-permute-done((bf16[32,1024]{1,0:T(8,128)(2,1)S(1)}, bf16[32,1024]{1,0:T(8,128)(2,1)S(1)}, u32[]{:S(2)}, u32[]{:S(2)}) %collective-permute-start.16) | collective-permute-done | bytes 65568 | tf_op jit(solution)/shard_map/ppermute | solution.py:549
  85.3 3.4 %copy-done = bf16[1024,4096]{1,0:T(8,128)(2,1)S(1)} copy-done((bf16[1024,4096]{1,0:T(8,128)(2,1)S(1)}, bf16[1024,4096]{1,0:T(8,128)(2,1)}, u32[]{:S(2)}) %copy-start) | copy-done | bytes 8388632
  88.7 3.4 %copy-done.1 = bf16[4096,1024]{1,0:T(8,128)(2,1)S(1)} copy-done((bf16[4096,1024]{1,0:T(8,128)(2,1)S(1)}, bf16[4096,1024]{1,0:T(8,128)(2,1)}, u32[]{:S(2)}) %copy-start.1) | copy-done | bytes 8388632
  92.1 11.8 %shard_map.135 = (bf16[32,1024]{1,0:T(8,128)(2,1)S(1)}, f32[8,128]{1,0:T(8,128)S(1)}) custom-call(s32[2]{0:T(128)S(1)} %fusion.1.counts, f32[32,1024]{1,0:T(8,128)S(1)} %get-tuple-element.73.x0, bf16[32,1024]{1,0:T(8,128)(2,1)S(1)} %collective-permute-done.15.x1, bf16[32,1024]{1,0:T(8,128)(2,1)S(1)} %collective-permute-done.16.x2, ...), custom_call_target="tpu_custom_call" | custom-call | bytes 1048576 | tf_op jit(solution)/shard_map/pallas_call | solution.py:357
  105.4 2.7 %collective-permute-start.18 = (bf16[32,1024]{1,0:T(8,128)(2,1)S(1)}, bf16[32,1024]{1,0:T(8,128)(2,1)S(1)}, u32[]{:S(2)}, u32[]{:S(2)}) collective-permute-start(bf16[32,1024]{1,0:T(8,128)(2,1)S(1)} %get-tuple-element.77.g0), channel_id=1, source_target_pairs={{0,2},{1,3},{2,0},{3,1},{4,6},{5,7},{6,4},{7,5},{8,10},{9,11},{10,... | collective-permute-start | bytes 196616 | tf_op jit(solution)/shard_map/ppermute | solution.py:549
  113.8 3.1 %collective-permute-done.22.d2 = bf16[128,256]{1,0:T(8,128)(2,1)S(1)} collective-permute-done((bf16[128,256]{1,0:T(8,128)(2,1)S(1)}, bf16[128,256]{1,0:T(8,128)(2,1)S(1)}, u32[]{:S(2)}, u32[]{:S(2)}) %collective-permute-start.22) | collective-permute-done | bytes 65568 | tf_op jit(solution)/shard_map/ppermute | solution.py:549
  117.9 3.5 %collective-permute-start.26 = (bf16[144,512]{1,0:T(8,128)(2,1)S(1)}, bf16[144,512]{1,0:T(8,128)(2,1)S(1)}, u32[]{:S(2)}, u32[]{:S(2)}) collective-permute-start(bf16[144,512]{1,0:T(8,128)(2,1)S(1)} %get-tuple-element.85), channel_id=1, source_target_pairs={{0,48},{16,32},{32,16},{48,0},{64,112},{80,96},{96,80},{112,64},{1... | collective-permute-start | bytes 442376 | tf_op jit(solution)/shard_map/ppermute | solution.py:537
  123.0 3.5 %collective-permute-done.26.refs_7_ = bf16[144,512]{1,0:T(8,128)(2,1)S(1)} collective-permute-done((bf16[144,512]{1,0:T(8,128)(2,1)S(1)}, bf16[144,512]{1,0:T(8,128)(2,1)S(1)}, u32[]{:S(2)}, u32[]{:S(2)}) %collective-permute-start.26) | collective-permute-done | bytes 147488 | tf_op jit(solution)/shard_map/ppermute | solution.py:537
  126.5 3.1 %collective-permute-done.25.refs_6_ = bf16[144,512]{1,0:T(8,128)(2,1)S(1)} collective-permute-done((bf16[144,512]{1,0:T(8,128)(2,1)S(1)}, bf16[144,512]{1,0:T(8,128)(2,1)S(1)}, u32[]{:S(2)}, u32[]{:S(2)}) %collective-permute-start.25) | collective-permute-done | bytes 147488 | tf_op jit(solution)/shard_map/ppermute | solution.py:537
  129.6 11.7 %shard_map.138 = (f32[4,128,512]{2,1,0:T(8,128)S(1)}, bf16[1024,256]{1,0:T(8,128)(2,1)S(1)}, bf16[1024,256]{1,0:T(8,128)(2,1)S(1)}) custom-call(s32[1]{0:T(128)} %bitcast.ctx, s32[4,128]{1,0:T(4,128)S(1)} %bitcast.7, bf16[128,512]{1,0:T(8,128)(2,1)S(1)} %copy-done.19, bf16[128,512]{1,0:T(8,128)(2,1)S(1)} %copy-done.31, bf16[128,512]{1,0:T(8,128)(2,1)S(1)} %copy-done.27, ...), custom_call_target="tpu_custom_call" | custom-call | flops 20000000000 | bytes 1048576 | tf_op jit(solution)/shard_map/pallas_call | solution.py:485
  141.3 11.7 %shard_map.139 = (bf16[128,512]{1,0:T(8,128)(2,1)S(1)}, bf16[128,512]{1,0:T(8,128)(2,1)S(1)}, bf16[128,512]{1,0:T(8,128)(2,1)S(1)}, bf16[128,512]{1,0:T(8,128)(2...) custom-call(s32[1]{0:T(128)} %bitcast.ctx, s32[4,128]{1,0:T(4,128)S(1)} %bitcast.8, ...), custom_call_target="tpu_custom_call" | custom-call | flops 20000000000 | bytes 1048576 | tf_op jit(solution)/shard_map/pallas_call | solution.py:485
  153.1 2.8 %collective-permute-start.30 = (bf16[1024,256]{1,0:T(8,128)(2,1)S(1)}, bf16[1024,256]{1,0:T(8,128)(2,1)S(1)}, u32[]{:S(2)}, u32[]{:S(2)}) collective-permute-start(bf16[1024,256]{1,0:T(8,128)(2,1)S(1)} %get-tuple-element.94), channel_id=1, source_target_pairs={{0,96},{16,112},{32,64},{48,80},{64,32},{80,48},{96,0},{112,16},{1... | collective-permute-start | bytes 1572872 | tf_op jit(solution)/shard_map/ppermute | solution.py:537
  166.9 21.0 %collective-permute-done.28.d2 = bf16[128,512]{1,0:T(8,128)(2,1)S(1)} collective-permute-done((bf16[128,512]{1,0:T(8,128)(2,1)S(1)}, bf16[128,512]{1,0:T(8,128)(2,1)S(1)}, u32[]{:S(2)}, u32[]{:S(2)}) %collective-permute-start.28) | collective-permute-done | bytes 131104 | tf_op jit(solution)/shard_map/ppermute | solution.py:537
  (128 shorter events, 54.1 us)
Async XLA Ops:
  3.6 20.3 %collective-permute-start.5 = (bf16[1024,256]{1,0:T(8,128)(2,1)S(1)}, bf16[1024,256]{1,0:T(8,128)(2,1)S(1)}, u32[]{:S(2)}, u32[]{:S(2)}) collective-permute-start(bf16[1024,256]{1,0:T(8,128)(2,1)S(1)} %get-tuple-element.57.refs_4_.refs_8_), channel_id=1, source_target_pairs={{0,96},{16,112},{32,64},{48,80},{64,32},{80,48},{96,0},{112,16},{1... | collective-permute-start | bytes 1572872 | tf_op jit(solution)/shard_map/ppermute | solution.py:537
  9.2 9.8 %collective-permute-start.2 = (bf16[128,512]{1,0:T(8,128)(2,1)S(1)}, bf16[128,512]{1,0:T(8,128)(2,1)S(1)}, u32[]{:S(2)}, u32[]{:S(2)}) collective-permute-start(bf16[128,512]{1,0:T(8,128)(2,1)S(1)} %get-tuple-element.54), channel_id=1, source_target_pairs={{0,48},{16,32},{32,16},{48,0},{64,112},{80,96},{96,80},{112,64},{1... | collective-permute-start | bytes 393224 | tf_op jit(solution)/shard_map/ppermute | solution.py:537
  12.8 9.8 %collective-permute-start.1 = (bf16[128,512]{1,0:T(8,128)(2,1)S(1)}, bf16[128,512]{1,0:T(8,128)(2,1)S(1)}, u32[]{:S(2)}, u32[]{:S(2)}) collective-permute-start(bf16[128,512]{1,0:T(8,128)(2,1)S(1)} %get-tuple-element.54), channel_id=1, source_target_pairs={{0,16},{16,0},{32,48},{48,32},{64,80},{80,64},{96,112},{112,96},{1... | collective-permute-start | bytes 393224 | tf_op jit(solution)/shard_map/ppermute | solution.py:537
  13.2 10.0 %collective-permute-start = (bf16[128,512]{1,0:T(8,128)(2,1)S(1)}, bf16[128,512]{1,0:T(8,128)(2,1)S(1)}, u32[]{:S(2)}, u32[]{:S(2)}) collective-permute-start(bf16[128,512]{1,0:T(8,128)(2,1)S(1)} %get-tuple-element.53.refs_0_), channel_id=1, source_target_pairs={{0,32},{16,48},{32,0},{48,16},{64,96},{80,112},{96,64},{112,80},{1... | collective-permute-start | bytes 393224 | tf_op jit(solution)/shard_map/ppermute | solution.py:537
  14.6 18.7 %collective-permute-start.4 = (bf16[1024,256]{1,0:T(8,128)(2,1)S(1)}, bf16[1024,256]{1,0:T(8,128)(2,1)S(1)}, u32[]{:S(2)}, u32[]{:S(2)}) collective-permute-start(bf16[1024,256]{1,0:T(8,128)(2,1)S(1)} %get-tuple-element.56), channel_id=1, source_target_pairs={{0,112},{16,96},{32,80},{48,64},{64,48},{80,32},{96,16},{112,0},{1... | collective-permute-start | bytes 1572872 | tf_op jit(solution)/shard_map/ppermute | solution.py:537
  19.6 24.3 %collective-permute-start.3 = (bf16[1024,256]{1,0:T(8,128)(2,1)S(1)}, bf16[1024,256]{1,0:T(8,128)(2,1)S(1)}, u32[]{:S(2)}, u32[]{:S(2)}) collective-permute-start(bf16[1024,256]{1,0:T(8,128)(2,1)S(1)} %get-tuple-element.56), channel_id=1, source_target_pairs={{0,16},{16,0},{32,48},{48,32},{64,80},{80,64},{96,112},{112,96},{1... | collective-permute-start | bytes 1572872 | tf_op jit(solution)/shard_map/ppermute | solution.py:537
  43.9 13.4 %collective-permute-start.12 = (bf16[256,1024]{1,0:T(8,128)(2,1)S(1)}, bf16[256,1024]{1,0:T(8,128)(2,1)S(1)}, u32[]{:S(2)}, u32[]{:S(2)}) collective-permute-start(bf16[256,1024]{1,0:T(8,128)(2,1)S(1)} %copy-done.2), channel_id=1, source_target_pairs={{0,8},{1,9},{2,10},{3,11},{4,12},{5,13},{6,14},{7,15},{8,0},{9,1},... | collective-permute-start | bytes 1572872 | tf_op jit(solution)/shard_map/ppermute | solution.py:549
  57.3 17.5 %collective-permute-start.13 = (bf16[256,1024]{1,0:T(8,128)(2,1)S(1)}, bf16[256,1024]{1,0:T(8,128)(2,1)S(1)}, u32[]{:S(2)}, u32[]{:S(2)}) collective-permute-start(bf16[256,1024]{1,0:T(8,128)(2,1)S(1)} %copy-done.2), channel_id=1, source_target_pairs={{0,1},{1,0},{2,3},{3,2},{4,5},{5,4},{6,7},{7,6},{8,9},{9,8},{10,11... | collective-permute-start | bytes 1572872 | tf_op jit(solution)/shard_map/ppermute | solution.py:549
  57.3 17.5 %collective-permute-start.14 = (bf16[256,1024]{1,0:T(8,128)(2,1)S(1)}, bf16[256,1024]{1,0:T(8,128)(2,1)S(1)}, u32[]{:S(2)}, u32[]{:S(2)}) collective-permute-start(bf16[256,1024]{1,0:T(8,128)(2,1)S(1)} %collective-permute-done.12.w2), channel_id=1, source_target_pairs={{0,1},{1,0},{2,3},{3,2},{4,5},{5,4},{6,7},{7,6},{8,9},{9,8},{10,11... | collective-permute-start | bytes 1572872 | tf_op jit(solution)/shard_map/ppermute | solution.py:549
  57.8 6.5 %collective-permute-start.6 = (bf16[144,512]{1,0:T(8,128)(2,1)}, bf16[144,512]{1,0:T(8,128)(2,1)S(1)}, u32[]{:S(2)}, u32[]{:S(2)}) collective-permute-start(bf16[144,512]{1,0:T(8,128)(2,1)} %get-tuple-element.63), channel_id=1, source_target_pairs={{0,32},{16,48},{32,0},{48,16},{64,96},{80,112},{96,64},{112,80},{1... | collective-permute-start | bytes 442376 | tf_op jit(solution)/shard_map/ppermute | solution.py:537
  58.2 10.6 %collective-permute-start.7 = (bf16[144,512]{1,0:T(8,128)(2,1)}, bf16[144,512]{1,0:T(8,128)(2,1)S(1)}, u32[]{:S(2)}, u32[]{:S(2)}) collective-permute-start(bf16[144,512]{1,0:T(8,128)(2,1)} %get-tuple-element.64), channel_id=1, source_target_pairs={{0,16},{16,0},{32,48},{48,32},{64,80},{80,64},{96,112},{112,96},{1... | collective-permute-start | bytes 442376 | tf_op jit(solution)/shard_map/ppermute | solution.py:537
  60.4 8.4 %collective-permute-start.8 = (bf16[144,512]{1,0:T(8,128)(2,1)S(1)}, bf16[144,512]{1,0:T(8,128)(2,1)S(1)}, u32[]{:S(2)}, u32[]{:S(2)}) collective-permute-start(bf16[144,512]{1,0:T(8,128)(2,1)S(1)} %get-tuple-element.65), channel_id=1, source_target_pairs={{0,48},{16,32},{32,16},{48,0},{64,112},{80,96},{96,80},{112,64},{1... | collective-permute-start | bytes 442376 | tf_op jit(solution)/shard_map/ppermute | solution.py:537
  77.0 6.5 %collective-permute-start.16 = (bf16[32,1024]{1,0:T(8,128)(2,1)S(1)}, bf16[32,1024]{1,0:T(8,128)(2,1)S(1)}, u32[]{:S(2)}, u32[]{:S(2)}) collective-permute-start(bf16[32,1024]{1,0:T(8,128)(2,1)S(1)} %get-tuple-element.75), channel_id=1, source_target_pairs={{0,4},{1,5},{2,6},{3,7},{4,0},{5,1},{6,2},{7,3},{8,12},{9,13},{10,... | collective-permute-start | bytes 196616 | tf_op jit(solution)/shard_map/ppermute | solution.py:549
  104.0 5.8 %collective-permute-start.20 = (bf16[32,1024]{1,0:T(8,128)(2,1)S(1)}, bf16[32,1024]{1,0:T(8,128)(2,1)S(1)}, u32[]{:S(2)}, u32[]{:S(2)}) collective-permute-start(bf16[32,1024]{1,0:T(8,128)(2,1)S(1)} %get-tuple-element.77.g0), channel_id=1, source_target_pairs={{0,6},{1,7},{2,4},{3,5},{4,2},{5,3},{6,0},{7,1},{8,14},{9,15},{10,... | collective-permute-start | bytes 196616 | tf_op jit(solution)/shard_map/ppermute | solution.py:549
  104.7 5.8 %collective-permute-start.19 = (bf16[32,1024]{1,0:T(8,128)(2,1)S(1)}, bf16[32,1024]{1,0:T(8,128)(2,1)S(1)}, u32[]{:S(2)}, u32[]{:S(2)}) collective-permute-start(bf16[32,1024]{1,0:T(8,128)(2,1)S(1)} %get-tuple-element.77.g0), channel_id=1, source_target_pairs={{0,4},{1,5},{2,6},{3,7},{4,0},{5,1},{6,2},{7,3},{8,12},{9,13},{10,... | collective-permute-start | bytes 196616 | tf_op jit(solution)/shard_map/ppermute | solution.py:549
  105.4 5.6 %collective-permute-start.18 = (bf16[32,1024]{1,0:T(8,128)(2,1)S(1)}, bf16[32,1024]{1,0:T(8,128)(2,1)S(1)}, u32[]{:S(2)}, u32[]{:S(2)}) collective-permute-start(bf16[32,1024]{1,0:T(8,128)(2,1)S(1)} %get-tuple-element.77.g0), channel_id=1, source_target_pairs={{0,2},{1,3},{2,0},{3,1},{4,6},{5,7},{6,4},{7,5},{8,10},{9,11},{10,... | collective-permute-start | bytes 196616 | tf_op jit(solution)/shard_map/ppermute | solution.py:549
  117.9 8.6 %collective-permute-start.26 = (bf16[144,512]{1,0:T(8,128)(2,1)S(1)}, bf16[144,512]{1,0:T(8,128)(2,1)S(1)}, u32[]{:S(2)}, u32[]{:S(2)}) collective-permute-start(bf16[144,512]{1,0:T(8,128)(2,1)S(1)} %get-tuple-element.85), channel_id=1, source_target_pairs={{0,48},{16,32},{32,16},{48,0},{64,112},{80,96},{96,80},{112,64},{1... | collective-permute-start | bytes 442376 | tf_op jit(solution)/shard_map/ppermute | solution.py:537
  121.4 8.1 %collective-permute-start.25 = (bf16[144,512]{1,0:T(8,128)(2,1)S(1)}, bf16[144,512]{1,0:T(8,128)(2,1)S(1)}, u32[]{:S(2)}, u32[]{:S(2)}) collective-permute-start(bf16[144,512]{1,0:T(8,128)(2,1)S(1)} %get-tuple-element.85), channel_id=1, source_target_pairs={{0,16},{16,0},{32,48},{48,32},{64,80},{80,64},{96,112},{112,96},{1... | collective-permute-start | bytes 442376 | tf_op jit(solution)/shard_map/ppermute | solution.py:537
  122.4 7.1 %collective-permute-start.24 = (bf16[144,512]{1,0:T(8,128)(2,1)S(1)}, bf16[144,512]{1,0:T(8,128)(2,1)S(1)}, u32[]{:S(2)}, u32[]{:S(2)}) collective-permute-start(bf16[144,512]{1,0:T(8,128)(2,1)S(1)} %get-tuple-element.84.refs_4_), channel_id=1, source_target_pairs={{0,32},{16,48},{32,0},{48,16},{64,96},{80,112},{96,64},{112,80},{1... | collective-permute-start | bytes 442376 | tf_op jit(solution)/shard_map/ppermute | solution.py:537
  153.1 36.1 %collective-permute-start.30 = (bf16[1024,256]{1,0:T(8,128)(2,1)S(1)}, bf16[1024,256]{1,0:T(8,128)(2,1)S(1)}, u32[]{:S(2)}, u32[]{:S(2)}) collective-permute-start(bf16[1024,256]{1,0:T(8,128)(2,1)S(1)} %get-tuple-element.94), channel_id=1, source_target_pairs={{0,96},{16,112},{32,64},{48,80},{64,32},{80,48},{96,0},{112,16},{1... | collective-permute-start | bytes 1572872 | tf_op jit(solution)/shard_map/ppermute | solution.py:537
  155.9 33.2 %collective-permute-start.31 = (bf16[1024,256]{1,0:T(8,128)(2,1)S(1)}, bf16[1024,256]{1,0:T(8,128)(2,1)S(1)}, u32[]{:S(2)}, u32[]{:S(2)}) collective-permute-start(bf16[1024,256]{1,0:T(8,128)(2,1)S(1)} %get-tuple-element.95), channel_id=1, source_target_pairs={{0,16},{16,0},{32,48},{48,32},{64,80},{80,64},{96,112},{112,96},{1... | collective-permute-start | bytes 1572872 | tf_op jit(solution)/shard_map/ppermute | solution.py:537
  157.4 31.7 %collective-permute-start.32 = (bf16[1024,256]{1,0:T(8,128)(2,1)S(1)}, bf16[1024,256]{1,0:T(8,128)(2,1)S(1)}, u32[]{:S(2)}, u32[]{:S(2)}) collective-permute-start(bf16[1024,256]{1,0:T(8,128)(2,1)S(1)} %get-tuple-element.96), channel_id=1, source_target_pairs={{0,112},{16,96},{32,80},{48,64},{64,48},{80,32},{96,16},{112,0},{1... | collective-permute-start | bytes 1572872 | tf_op jit(solution)/shard_map/ppermute | solution.py:537
  159.8 28.0 %collective-permute-start.28 = (bf16[128,512]{1,0:T(8,128)(2,1)S(1)}, bf16[128,512]{1,0:T(8,128)(2,1)S(1)}, u32[]{:S(2)}, u32[]{:S(2)}) collective-permute-start(bf16[128,512]{1,0:T(8,128)(2,1)S(1)} %get-tuple-element.89), channel_id=1, source_target_pairs={{0,16},{16,0},{32,48},{48,32},{64,80},{80,64},{96,112},{112,96},{1... | collective-permute-start | bytes 393224 | tf_op jit(solution)/shard_map/ppermute | solution.py:537
  164.3 23.5 %collective-permute-start.29 = (bf16[128,512]{1,0:T(8,128)(2,1)S(1)}, bf16[128,512]{1,0:T(8,128)(2,1)S(1)}, u32[]{:S(2)}, u32[]{:S(2)}) collective-permute-start(bf16[128,512]{1,0:T(8,128)(2,1)S(1)} %get-tuple-element.90), channel_id=1, source_target_pairs={{0,48},{16,32},{32,16},{48,0},{64,112},{80,96},{96,80},{112,64},{1... | collective-permute-start | bytes 393224 | tf_op jit(solution)/shard_map/ppermute | solution.py:537
  (42 other events, 525.0 us)
where the time goes:
time: 192 us; the launch traced here: 191 us
  waiting for transfers between devices  65.7 us (34%)
  Pallas kernels  55.8 us (29%)
  starting transfers between devices  50.2 us (26%)
  local copies, waits for them, and re-layouts  17.4 us (9%)
    ppermute x18, waiting for transfers between devices, send_ctx(): return lax.ppermute(array, 'ctx', ctx_swap(turn, flip))  46.3 us
    ppermute x18, starting transfers between devices, send_ctx(): return lax.ppermute(array, 'ctx', ctx_swap(turn, flip))  35.8 us
    pallas_call x2, Pallas kernels, backward(): call(functools.partial(backward_kernel, blocks=blocks, starts=starts, fir...  23.4 us
    ppermute x15, waiting for transfers between devices, send_frame(): return array if mask == 0 else lax.ppermute(array, 'frame', frame_xor(mask))  19.5 us
    unnamed x66, local copies, waits for them, and re-layouts  16.8 us
    ppermute x15, starting transfers between devices, send_frame(): return array if mask == 0 else lax.ppermute(array, 'frame', frame_xor(mask))  14.3 us
    pallas_call x2, Pallas kernels, forward(): call(functools.partial(forward_kernel, blocks=blocks, starts=starts, firs...  13.1 us
    pallas_call x1, Pallas kernels, reward_call(): call(reward_kernel, [SMEM] + [VMEM] * 7, [((rows, vision), bf16), ((8, HD...  11.8 us
  transfers between devices with their start and end apart: 33, of which 17 were waited for; matrix products, arithmetic and copies ran while one was open for 1% of the time, Pallas kernels for 8%

commit v1 on v0

--- a/solution.py
+++ b/solution.py
@@ -42,7 +42,7 @@
         in_specs=in_specs,
         out_specs=[VMEM] * len(outs),
         scratch_shapes=list(scratch),
-        compiler_params=pltpu.CompilerParams(vmem_limit_bytes=24 * 1024 * 1024),
+        compiler_params=pltpu.CompilerParams(vmem_limit_bytes=16 * 1024 * 1024),
     )
 
 
@@ -128,7 +128,7 @@
         kaug[part * rows : part * rows + rows, HD:] = jnp.where(lane == 6, bias, ones).astype(bf16)
 
 
-def forward_kernel(ctx, counts, *refs, blocks, starts, first):
+def forward_kernel(ctx, counts, *refs, blocks, starts, first, last, extras):
     refs = list(refs)
 
     def take(count):
@@ -141,12 +141,13 @@
     kv_refs = take(pieces)
     if not first:
         acc_in, stat_in = take(2)
-    if first:
+    take(extras)
+    if last:
+        out_refs = take(blocks)
+    else:
         acc_out, stat_out = take(2)
-    else:
-        out_refs = take(blocks)
     kaug, v_t, q_all, *scores = take(5)
-    if not first:
+    if last:
         (out_all,) = take(1)
     rows = kv_refs[0].shape[0]
     keys = pieces * rows
@@ -183,7 +184,7 @@
             p = jnp.exp2((scores[slot][span, :] - top) * EXP2_SCALE)
             total = total + jnp.sum(p, axis=0, keepdims=True)
             acc = acc + dot(v_t[:, span], p.astype(bf16), NN)
-        if first:
+        if not last:
             acc_out[i] = acc
             which = lax.broadcasted_iota(jnp.int32, (8, wide), 0)
             stat_out[i] = jnp.where(which == 0, top, total)
@@ -204,23 +205,29 @@
         return block(2 * t + 1, 1, middle, jnp.minimum(2 * t + 2, blocks - 1))
 
     lax.fori_loop(0, blocks // 2, pair, top)
-    if not first:
+    if last:
         for i in range(blocks):
             out_refs[i][...] = out_all[i]
 
 
-def forward(ctx, counts, q_blocks, kv_pieces, starts, before=None):
+def forward(ctx, counts, q_blocks, kv_pieces, starts, before=(), last=False, extras=()):
     blocks = len(q_blocks)
     wide = q_blocks[0].shape[1]
     keys = len(kv_pieces) * kv_pieces[0].shape[0]
-    first = before is None
-    if first:
+    if last:
+        outs = [((HD + EXTRA, wide), bf16)] * blocks
+    else:
         outs = [((blocks, HD, wide), f32), ((blocks, 8, wide), f32)]
-    else:
-        outs = [((HD + EXTRA, wide), bf16)] * blocks
-    args = [*q_blocks, *kv_pieces] + ([] if first else list(before))
+    args = [*q_blocks, *kv_pieces, *before, *extras]
     return call(
-        functools.partial(forward_kernel, blocks=blocks, starts=starts, first=first),
+        functools.partial(
+            forward_kernel,
+            blocks=blocks,
+            starts=starts,
+            first=not before,
+            last=last,
+            extras=len(extras),
+        ),
         [SMEM] + [VMEM] * (len(args) + 1),
         outs,
         [
@@ -230,7 +237,7 @@
             pltpu.VMEM((keys, wide), f32),
             pltpu.VMEM((keys, wide), f32),
         ]
-        + ([] if first else [pltpu.VMEM((blocks, HD + EXTRA, wide), bf16)]),
+        + ([pltpu.VMEM((blocks, HD + EXTRA, wide), bf16)] if last else []),
         work=10**10,
     )(ctx, counts, *args)
 
@@ -458,13 +465,12 @@
             ref[:, HD:] = dv[where, :].astype(bf16)
 
 
-def backward(ctx, counts, q_blocks, g_blocks, kv_pieces, starts, before=None):
+def backward(ctx, counts, q_blocks, g_blocks, kv_pieces, starts, before=None, last=False):
     blocks = len(q_blocks)
     pieces = len(kv_pieces)
     wide = q_blocks[0].shape[1]
     rows = kv_pieces[0].shape[0]
     keys = pieces * rows
-    last = before is not None
     packed = ((rows, 2 * HD), bf16)
     if last:
         outs = [((HD, wide), bf16)] * blocks + [((rows, HD), f32)] * 2 + [packed] * (pieces - 1)
@@ -481,10 +487,10 @@
     ]
     if last:
         scratch.append(pltpu.VMEM((blocks, HD, wide), bf16))
-    args = [*q_blocks, *g_blocks, *kv_pieces] + ([before] if last else [])
+    args = [*q_blocks, *g_blocks, *kv_pieces] + ([] if before is None else [before])
     out = call(
         functools.partial(
-            backward_kernel, blocks=blocks, starts=starts, first=not last, last=last
+            backward_kernel, blocks=blocks, starts=starts, first=before is None, last=last
         ),
         [SMEM] + [VMEM] * (len(args) + 1),
         outs,
@@ -592,7 +598,6 @@
     q_blocks = exchange((qs, qs, qo, qo))
     kv_send, _ = lax.optimization_barrier((kv_send, qs))
     kv_par = send_ctx(kv_send, 0, 1)
-    kv_far_par = send_ctx(kv_send, 2, 1)
 
     slot_index = jnp.arange(frame_slots, dtype=jnp.int32)
     same_clip = clip_of_frame[:, None] == clip_of_frame[None, :]
@@ -607,12 +612,12 @@
     mine = slot_place[None, :] == jnp.arange(CLIP, dtype=jnp.int32)[:, None]
     my_counts = jnp.sum(jnp.where(mine, slot_counts[None, :], 0), axis=1).astype(jnp.int32)
 
-    before = forward(ctx, counts, q_blocks, (kv_own, kv_far), (0, 2))
-    kv_par, kv_far_par, in_proj, _ = lax.optimization_barrier(
-        (kv_par, kv_far_par, in_proj, before[1])
-    )
+    state = forward(ctx, counts, q_blocks, (kv_own, kv_far), (0, 2))
+    kv_par, in_proj, _ = lax.optimization_barrier((kv_par, in_proj, state[1]))
+    kv_far_par = send_ctx(kv_par, 2, 0)
     near = send_frame(in_proj, 8)
-    partial = forward(ctx, counts, q_blocks, (kv_par, kv_far_par), (1, 3), before)
+    state = forward(ctx, counts, q_blocks, (kv_par,), (1,), state)
+    partial = forward(ctx, counts, q_blocks, (kv_far_par,), (3,), state, True)
     in_proj, near_late, _ = lax.optimization_barrier((in_proj, near, partial[0]))
     weights = (in_proj, send_frame(in_proj, 1), near_late, send_frame(near_late, 1))
     partial = exchange(partial)
@@ -622,6 +627,7 @@
         combine_kernel,
         [SMEM] + [VMEM] * 5,
         [((width, query_rows), bf16), ((2, 8, query_rows), f32)] + [((quarter, width), bf16)] * 4,
+        work=5 * 10**9,
     )(ctx, place, *partial)
     chunks = [send_frame(chunk, mask) for chunk, mask in zip(chunks, QUAD_MASKS)]
     vision = in_proj.shape[1]
@@ -630,6 +636,7 @@
         project_kernel,
         [VMEM] * 8,
         [((clip_rows, vision), f32)] + [((clip_rows, vision), bf16)] * 3,
+        work=5 * 10**9,
     )(*chunks, *weights)
     inputs = [send_frame(x, mask) for x, mask in zip(inputs, Y_MASKS)]
     input_grad, reward = reward_call(my_counts, inputs, reward_head, mlp_up, mlp_down)
@@ -649,13 +656,15 @@
         [pltpu.VMEM((query_rows, width), bf16)],
     )(ctx, place, *grads, out_t, logs)
     g_blocks = exchange((gs, gs, go, go))
-    dq, (d_par, d_far_par) = backward(ctx, counts, q_blocks, g_blocks, (kv_par, kv_far_par), (1, 3))
+    dq, (d_far_par,) = backward(ctx, counts, q_blocks, g_blocks, (kv_far_par,), (3,))
+    d_far_par = send_ctx(d_far_par, 2, 1)
+    dq, (d_par,) = backward(ctx, counts, q_blocks, g_blocks, (kv_par,), (1,), dq)
     d_par = send_ctx(d_par, 0, 1)
-    d_far_par = send_ctx(d_far_par, 2, 1)
-    dq, (dk_own, dv_own, d_far) = backward(
-        ctx, counts, q_blocks, g_blocks, (kv_own, kv_far), (0, 2), dq
+    dq, (d_far,) = backward(ctx, counts, q_blocks, g_blocks, (kv_far,), (2,), dq)
+    d_far = send_ctx(d_far, 2, 0)
+    dq, (dk_own, dv_own) = backward(
+        ctx, counts, q_blocks, g_blocks, (kv_own,), (0,), dq, True
     )
-    d_far = send_ctx(d_far, 2, 0)
     dq = exchange(dq)
     (query_grad,) = call(
         query_grad_kernel,

time: 192 us -> 175 us (0.911)
  waiting for transfers between devices: 65.7 us -> 55.6 us
  local copies, waits for them, and re-layouts: 17.4 us -> 8.44 us
  Pallas kernels: 55.8 us -> 59.1 us
  starting transfers between devices: 50.2 us -> 47.8 us
    unnamed x66 -> x50, local copies, waits for them, and re-layouts: 16.8 us -> 7.85 us
    ppermute x18, waiting for transfers between devices: 46.3 us -> 40.7 us  [send_ctx(): return lax.ppermute(array, 'ctx', ctx_swap(turn, flip))]
    ppermute x15, waiting for transfers between devices: 19.5 us -> 14.9 us  [send_frame(): return array if mask == 0 else lax.ppermute(array, 'frame', frame_xor(mask))]
    ppermute x18, starting transfers between devices: 35.8 us -> 32.5 us  [send_ctx(): return lax.ppermute(array, 'ctx', ctx_swap(turn, flip))]
    pallas_call x2 -> x4, Pallas kernels: 23.4 us -> 24.9 us  [backward(): call(functools.partial(backward_kernel, blocks=blocks, starts=starts, fir...]
    pallas_call x2 -> x3, Pallas kernels: 13.1 us -> 13.9 us  [forward(): call(functools.partial(forward_kernel, blocks=blocks, starts=starts, firs...]
  transfers between devices with their start and end apart: 33 -> 33, of which waited for: 17 -> 19; matrix products, arithmetic and copies ran while one was open for 1% -> 1% of each run, Pallas kernels for 8% -> 14%
where the time goes in v1:
time: 175 us; the launch traced here: 174 us
  Pallas kernels  59.1 us (34%)
  waiting for transfers between devices  55.6 us (32%)
  starting transfers between devices  47.8 us (27%)
  local copies, waits for them, and re-layouts  8.44 us (5%)
  other arithmetic  1.95 us (1%)
    ppermute x18, waiting for transfers between devices, send_ctx(): return lax.ppermute(array, 'ctx', ctx_swap(turn, flip))  40.7 us
    ppermute x18, starting transfers between devices, send_ctx(): return lax.ppermute(array, 'ctx', ctx_swap(turn, flip))  32.5 us
    pallas_call x4, Pallas kernels, backward(): call(functools.partial(backward_kernel, blocks=blocks, starts=starts, fir...  24.9 us
    ppermute x15, starting transfers between devices, send_frame(): return array if mask == 0 else lax.ppermute(array, 'frame', frame_xor(mask))  15.3 us
    ppermute x15, waiting for transfers between devices, send_frame(): return array if mask == 0 else lax.ppermute(array, 'frame', frame_xor(mask))  14.9 us
    pallas_call x3, Pallas kernels, forward(): call(functools.partial(forward_kernel, blocks=blocks, starts=starts, firs...  13.9 us
    pallas_call x1, Pallas kernels, reward_call(): call(reward_kernel, [SMEM] + [VMEM] * 7, [((rows, vision), bf16), ((8, HD...  11.8 us
    unnamed x50, local copies, waits for them, and re-layouts  7.85 us
  transfers between devices with their start and end apart: 33, of which 19 were waited for; matrix products, arithmetic and copies ran while one was open for 1% of the time, Pallas kernels for 14%

profile of v1, /device:TPU:0, one launch (start us, length us, event | category | flops | bytes accessed | tf_op | source)
XLA Modules:
  0.0 173.9 jit_solution(992641798210784629)
XLA Ops:
  3.6 2.9 %collective-permute-start.4 = (bf16[1024,256]{1,0:T(8,128)(2,1)S(1)}, bf16[1024,256]{1,0:T(8,128)(2,1)S(1)}, u32[]{:S(2)}, u32[]{:S(2)}) collective-permute-start(bf16[1024,256]{1,0:T(8,128)(2,1)S(1)} %get-tuple-element.60.refs_4_.refs_8_), channel_id=1, source_target_pairs={{0,96},{16,112},{32,64},{48,80},{64,32},{80,48},{96,0},{112,16},{1... | collective-permute-start | bytes 1572872 | tf_op jit(solution)/shard_map/ppermute | solution.py:543
  9.2 3.6 %collective-permute-start.2 = (bf16[128,512]{1,0:T(8,128)(2,1)S(1)}, bf16[128,512]{1,0:T(8,128)(2,1)S(1)}, u32[]{:S(2)}, u32[]{:S(2)}) collective-permute-start(bf16[128,512]{1,0:T(8,128)(2,1)S(1)} %get-tuple-element.57), channel_id=1, source_target_pairs={{0,48},{16,32},{32,16},{48,0},{64,112},{80,96},{96,80},{112,64},{1... | collective-permute-start | bytes 393224 | tf_op jit(solution)/shard_map/ppermute | solution.py:543
  14.6 3.5 %collective-permute-start.3 = (bf16[1024,256]{1,0:T(8,128)(2,1)S(1)}, bf16[1024,256]{1,0:T(8,128)(2,1)S(1)}, u32[]{:S(2)}, u32[]{:S(2)}) collective-permute-start(bf16[1024,256]{1,0:T(8,128)(2,1)S(1)} %get-tuple-element.59), channel_id=1, source_target_pairs={{0,16},{16,0},{32,48},{48,32},{64,80},{80,64},{96,112},{112,96},{1... | collective-permute-start | bytes 1572872 | tf_op jit(solution)/shard_map/ppermute | solution.py:543
  21.4 6.0 %shard_map.131 = (f32[4,128,512]{2,1,0:T(8,128)S(1)}, f32[4,8,512]{2,1,0:T(8,128)S(1)}) custom-call(s32[1]{0:T(128)} %bitcast.ctx, s32[4,128]{1,0:T(4,128)S(1)} %bitcast.9, bf16[128,512]{1,0:T(8,128)(2,1)S(1)} %get-tuple-element.56.refs_0_, bf16[128,512]{1,0:T(8,128)(2,1)S(1)} %collective-permute-done.refs_1_, ...), custom_call_target="tpu_custom_call" | custom-call | flops 10000000000 | bytes 1048576 | tf_op jit(solution)/shard_map/pallas_call | solution.py:222
  27.4 3.2 %collective-permute-done.3.refs_4_.refs_8_ = bf16[1024,256]{1,0:T(8,128)(2,1)S(1)} collective-permute-done((bf16[1024,256]{1,0:T(8,128)(2,1)S(1)}, bf16[1024,256]{1,0:T(8,128)(2,1)S(1)}, u32[]{:S(2)}, u32[]{:S(2)}) %collective-permute-start.3) | collective-permute-done | bytes 524320 | tf_op jit(solution)/shard_map/ppermute | solution.py:543
  34.9 3.6 %shard_map.132 = (f32[4,128,512]{2,1,0:T(8,128)S(1)}, f32[4,8,512]{2,1,0:T(8,128)S(1)}) custom-call(s32[1]{0:T(128)} %bitcast.ctx, s32[4,128]{1,0:T(4,128)S(1)} %bitcast.10, bf16[128,512]{1,0:T(8,128)(2,1)S(1)} %get-tuple-element.56.refs_0_, bf16[128,512]{1,0:T(8,128)(2,1)S(1)} %copy-done.17, bf16[128,512]{1,0:T(8,128)(2,1)S(1)} %copy-done.14, ...), custom_call_target="tpu_custom_call" | custom-call | flops 10000000000 | bytes 1048576 | tf_op jit(solution)/shard_map/pallas_call | solution.py:222
  38.4 8.7 %collective-permute-done.5.refs_4_.refs_8_ = bf16[1024,256]{1,0:T(8,128)(2,1)S(1)} collective-permute-done((bf16[1024,256]{1,0:T(8,128)(2,1)S(1)}, bf16[1024,256]{1,0:T(8,128)(2,1)S(1)}, u32[]{:S(2)}, u32[]{:S(2)}) %collective-permute-start.5) | collective-permute-done | bytes 524320 | tf_op jit(solution)/shard_map/ppermute | solution.py:543
  47.1 4.3 %shard_map.133 = (bf16[144,512]{1,0:T(8,128)(2,1)S(1)}, bf16[144,512]{1,0:T(8,128)(2,1)}, bf16[144,512]{1,0:T(8,128)(2,1)}, bf16[144,512]{1,0:T(8,128)(2,1)}) custom-call(s32[1]{0:T(128)} %bitcast.ctx, s32[4,128]{1,0:T(4,128)S(1)} %bitcast.11, bf16[128,512]{1,0:T(8,128)(2,1)S(1)} %get-tuple-element.56.refs_0_, bf16[128,512]{1,0:T(8,128)(2,1)S(1)} %copy-done.17, ...), custom_call_target="tpu_custom_call" | custom-call | flops 10000000000 | bytes 1048576 | tf_op jit(solution)/shard_map/pallas_call | solution.py:222
  52.1 2.6 %collective-permute-start.7 = (bf16[144,512]{1,0:T(8,128)(2,1)}, bf16[144,512]{1,0:T(8,128)(2,1)}, u32[]{:S(2)}, u32[]{:S(2)}) collective-permute-start(bf16[144,512]{1,0:T(8,128)(2,1)} %get-tuple-element.68), channel_id=1, source_target_pairs={{0,16},{16,0},{32,48},{48,32},{64,80},{80,64},{96,112},{112,96},{1... | collective-permute-start | bytes 442376 | tf_op jit(solution)/shard_map/ppermute | solution.py:543
  67.2 3.0 %collective-permute-done.10.o2 = bf16[128,256]{1,0:T(8,128)(2,1)S(1)} collective-permute-done((bf16[128,256]{1,0:T(8,128)(2,1)S(1)}, bf16[128,256]{1,0:T(8,128)(2,1)S(1)}, u32[]{:S(2)}, u32[]{:S(2)}) %collective-permute-start.10) | collective-permute-done | bytes 65568 | tf_op jit(solution)/shard_map/ppermute | solution.py:555
  72.7 2.9 %collective-permute-start.16 = (bf16[32,1024]{1,0:T(8,128)(2,1)S(1)}, bf16[32,1024]{1,0:T(8,128)(2,1)S(1)}, u32[]{:S(2)}, u32[]{:S(2)}) collective-permute-start(bf16[32,1024]{1,0:T(8,128)(2,1)S(1)} %get-tuple-element.79), channel_id=1, source_target_pairs={{0,4},{1,5},{2,6},{3,7},{4,0},{5,1},{6,2},{7,3},{8,12},{9,13},{10,... | collective-permute-start | bytes 196616 | tf_op jit(solution)/shard_map/ppermute | solution.py:555
  75.9 3.4 %collective-permute-done.16.x2 = bf16[32,1024]{1,0:T(8,128)(2,1)S(1)} collective-permute-done((bf16[32,1024]{1,0:T(8,128)(2,1)S(1)}, bf16[32,1024]{1,0:T(8,128)(2,1)S(1)}, u32[]{:S(2)}, u32[]{:S(2)}) %collective-permute-start.16) | collective-permute-done | bytes 65568 | tf_op jit(solution)/shard_map/ppermute | solution.py:555
  81.1 11.8 %shard_map.136 = (bf16[32,1024]{1,0:T(8,128)(2,1)S(1)}, f32[8,128]{1,0:T(8,128)S(1)}) custom-call(s32[2]{0:T(128)S(1)} %fusion.1.counts, f32[32,1024]{1,0:T(8,128)S(1)} %get-tuple-element.77.x0, bf16[32,1024]{1,0:T(8,128)(2,1)S(1)} %collective-permute-done.15.x1, bf16[32,1024]{1,0:T(8,128)(2,1)S(1)} %collective-permute-done.16.x2, ...), custom_call_target="tpu_custom_call" | custom-call | bytes 1048576 | tf_op jit(solution)/shard_map/pallas_call | solution.py:364
  102.8 3.2 %collective-permute-done.22.d2 = bf16[128,256]{1,0:T(8,128)(2,1)S(1)} collective-permute-done((bf16[128,256]{1,0:T(8,128)(2,1)S(1)}, bf16[128,256]{1,0:T(8,128)(2,1)S(1)}, u32[]{:S(2)}, u32[]{:S(2)}) %collective-permute-start.22) | collective-permute-done | bytes 65568 | tf_op jit(solution)/shard_map/ppermute | solution.py:555
  106.8 3.0 %collective-permute-start.26 = (bf16[144,512]{1,0:T(8,128)(2,1)S(1)}, bf16[144,512]{1,0:T(8,128)(2,1)S(1)}, u32[]{:S(2)}, u32[]{:S(2)}) collective-permute-start(bf16[144,512]{1,0:T(8,128)(2,1)S(1)} %get-tuple-element.89), channel_id=1, source_target_pairs={{0,48},{16,32},{32,16},{48,0},{64,112},{80,96},{96,80},{112,64},{1... | collective-permute-start | bytes 442376 | tf_op jit(solution)/shard_map/ppermute | solution.py:543
  111.9 3.9 %collective-permute-done.26.refs_7_ = bf16[144,512]{1,0:T(8,128)(2,1)S(1)} collective-permute-done((bf16[144,512]{1,0:T(8,128)(2,1)S(1)}, bf16[144,512]{1,0:T(8,128)(2,1)S(1)}, u32[]{:S(2)}, u32[]{:S(2)}) %collective-permute-start.26) | collective-permute-done | bytes 147488 | tf_op jit(solution)/shard_map/ppermute | solution.py:543
  115.8 2.8 %collective-permute-done.25.refs_6_ = bf16[144,512]{1,0:T(8,128)(2,1)S(1)} collective-permute-done((bf16[144,512]{1,0:T(8,128)(2,1)S(1)}, bf16[144,512]{1,0:T(8,128)(2,1)S(1)}, u32[]{:S(2)}, u32[]{:S(2)}) %collective-permute-start.25) | collective-permute-done | bytes 147488 | tf_op jit(solution)/shard_map/ppermute | solution.py:543
  118.6 6.2 %shard_map.139 = (f32[4,128,512]{2,1,0:T(8,128)S(1)}, bf16[1024,256]{1,0:T(8,128)(2,1)S(1)}) custom-call(s32[1]{0:T(128)} %bitcast.ctx, s32[4,128]{1,0:T(4,128)S(1)} %bitcast.12, bf16[128,512]{1,0:T(8,128)(2,1)S(1)} %copy-done.10, bf16[128,512]{1,0:T(8,128)(2,1)S(1)} %copy-done.18, bf16[128,512]{1,0:T(8,128)(2,1)S(1)} %copy-done.15, ...), custom_call_target="tpu_custom_call" | custom-call | flops 20000000000 | bytes 1048576 | tf_op jit(solution)/shard_map/pallas_call | solution.py:491
  124.8 6.2 %shard_map.140 = (f32[4,128,512]{2,1,0:T(8,128)S(1)}, bf16[1024,256]{1,0:T(8,128)(2,1)S(1)}) custom-call(s32[1]{0:T(128)} %bitcast.ctx, s32[4,128]{1,0:T(4,128)S(1)} %bitcast.13, bf16[128,512]{1,0:T(8,128)(2,1)S(1)} %copy-done.10, bf16[128,512]{1,0:T(8,128)(2,1)S(1)} %copy-done.18, bf16[128,512]{1,0:T(8,128)(2,1)S(1)} %copy-done.15, ...), custom_call_target="tpu_custom_call" | custom-call | flops 20000000000 | bytes 1048576 | tf_op jit(solution)/shard_map/pallas_call | solution.py:491
  131.0 6.2 %shard_map.141 = (f32[4,128,512]{2,1,0:T(8,128)S(1)}, bf16[1024,256]{1,0:T(8,128)(2,1)S(1)}) custom-call(s32[1]{0:T(128)} %bitcast.ctx, s32[4,128]{1,0:T(4,128)S(1)} %bitcast.14, bf16[128,512]{1,0:T(8,128)(2,1)S(1)} %copy-done.10, bf16[128,512]{1,0:T(8,128)(2,1)S(1)} %copy-done.18, bf16[128,512]{1,0:T(8,128)(2,1)S(1)} %copy-done.15, ...), custom_call_target="tpu_custom_call" | custom-call | flops 20000000000 | bytes 1048576 | tf_op jit(solution)/shard_map/pallas_call | solution.py:491
  140.1 3.4 %collective-permute-start.32 = (bf16[1024,256]{1,0:T(8,128)(2,1)S(1)}, bf16[1024,256]{1,0:T(8,128)(2,1)S(1)}, u32[]{:S(2)}, u32[]{:S(2)}) collective-permute-start(bf16[1024,256]{1,0:T(8,128)(2,1)S(1)} %get-tuple-element.102), channel_id=1, source_target_pairs={{0,112},{16,96},{32,80},{48,64},{64,48},{80,32},{96,16},{112,0},{1... | collective-permute-start | bytes 1572872 | tf_op jit(solution)/shard_map/ppermute | solution.py:543
  143.5 6.2 %shard_map.142 = (bf16[128,512]{1,0:T(8,128)(2,1)S(1)}, bf16[128,512]{1,0:T(8,128)(2,1)S(1)}, bf16[128,512]{1,0:T(8,128)(2,1)S(1)}, bf16[128,512]{1,0:T(8,128)(2...) custom-call(s32[1]{0:T(128)} %bitcast.ctx, s32[4,128]{1,0:T(4,128)S(1)} %bitcast.15, ...), custom_call_target="tpu_custom_call" | custom-call | flops 20000000000 | bytes 1048576 | tf_op jit(solution)/shard_map/pallas_call | solution.py:491
  152.0 2.8 %collective-permute-done.27.d1 = bf16[128,512]{1,0:T(8,128)(2,1)S(1)} collective-permute-done((bf16[128,512]{1,0:T(8,128)(2,1)S(1)}, bf16[128,512]{1,0:T(8,128)(2,1)S(1)}, u32[]{:S(2)}, u32[]{:S(2)}) %collective-permute-start.27) | collective-permute-done | bytes 131104 | tf_op jit(solution)/shard_map/ppermute | solution.py:543
  156.9 13.6 %collective-permute-done.28.d2 = bf16[128,512]{1,0:T(8,128)(2,1)S(1)} collective-permute-done((bf16[128,512]{1,0:T(8,128)(2,1)S(1)}, bf16[128,512]{1,0:T(8,128)(2,1)S(1)}, u32[]{:S(2)}, u32[]{:S(2)}) %collective-permute-start.28) | collective-permute-done | bytes 131104 | tf_op jit(solution)/shard_map/ppermute | solution.py:543
  (117 shorter events, 55.7 us)
Async XLA Ops:
  3.6 17.1 %collective-permute-start.4 = (bf16[1024,256]{1,0:T(8,128)(2,1)S(1)}, bf16[1024,256]{1,0:T(8,128)(2,1)S(1)}, u32[]{:S(2)}, u32[]{:S(2)}) collective-permute-start(bf16[1024,256]{1,0:T(8,128)(2,1)S(1)} %get-tuple-element.60.refs_4_.refs_8_), channel_id=1, source_target_pairs={{0,96},{16,112},{32,64},{48,80},{64,32},{80,48},{96,0},{112,16},{1... | collective-permute-start | bytes 1572872 | tf_op jit(solution)/shard_map/ppermute | solution.py:543
  9.2 10.5 %collective-permute-start.2 = (bf16[128,512]{1,0:T(8,128)(2,1)S(1)}, bf16[128,512]{1,0:T(8,128)(2,1)S(1)}, u32[]{:S(2)}, u32[]{:S(2)}) collective-permute-start(bf16[128,512]{1,0:T(8,128)(2,1)S(1)} %get-tuple-element.57), channel_id=1, source_target_pairs={{0,48},{16,32},{32,16},{48,0},{64,112},{80,96},{96,80},{112,64},{1... | collective-permute-start | bytes 393224 | tf_op jit(solution)/shard_map/ppermute | solution.py:543
  12.8 7.9 %collective-permute-start.1 = (bf16[128,512]{1,0:T(8,128)(2,1)S(1)}, bf16[128,512]{1,0:T(8,128)(2,1)S(1)}, u32[]{:S(2)}, u32[]{:S(2)}) collective-permute-start(bf16[128,512]{1,0:T(8,128)(2,1)S(1)} %get-tuple-element.57), channel_id=1, source_target_pairs={{0,16},{16,0},{32,48},{48,32},{64,80},{80,64},{96,112},{112,96},{1... | collective-permute-start | bytes 393224 | tf_op jit(solution)/shard_map/ppermute | solution.py:543
  13.2 7.4 %collective-permute-start = (bf16[128,512]{1,0:T(8,128)(2,1)S(1)}, bf16[128,512]{1,0:T(8,128)(2,1)S(1)}, u32[]{:S(2)}, u32[]{:S(2)}) collective-permute-start(bf16[128,512]{1,0:T(8,128)(2,1)S(1)} %get-tuple-element.56.refs_0_), channel_id=1, source_target_pairs={{0,32},{16,48},{32,0},{48,16},{64,96},{80,112},{96,64},{112,80},{1... | collective-permute-start | bytes 393224 | tf_op jit(solution)/shard_map/ppermute | solution.py:543
  14.6 16.1 %collective-permute-start.3 = (bf16[1024,256]{1,0:T(8,128)(2,1)S(1)}, bf16[1024,256]{1,0:T(8,128)(2,1)S(1)}, u32[]{:S(2)}, u32[]{:S(2)}) collective-permute-start(bf16[1024,256]{1,0:T(8,128)(2,1)S(1)} %get-tuple-element.59), channel_id=1, source_target_pairs={{0,16},{16,0},{32,48},{48,32},{64,80},{80,64},{96,112},{112,96},{1... | collective-permute-start | bytes 1572872 | tf_op jit(solution)/shard_map/ppermute | solution.py:543
  30.7 26.6 %collective-permute-start.12 = (bf16[256,1024]{1,0:T(8,128)(2,1)S(1)}, bf16[256,1024]{1,0:T(8,128)(2,1)S(1)}, u32[]{:S(2)}, u32[]{:S(2)}) collective-permute-start(bf16[256,1024]{1,0:T(8,128)(2,1)S(1)} %copy-done.2), channel_id=1, source_target_pairs={{0,8},{1,9},{2,10},{3,11},{4,12},{5,13},{6,14},{7,15},{8,0},{9,1},... | collective-permute-start | bytes 1572872 | tf_op jit(solution)/shard_map/ppermute | solution.py:555
  32.6 14.6 %collective-permute-start.5 = (bf16[1024,256]{1,0:T(8,128)(2,1)S(1)}, bf16[1024,256]{1,0:T(8,128)(2,1)S(1)}, u32[]{:S(2)}, u32[]{:S(2)}) collective-permute-start(bf16[1024,256]{1,0:T(8,128)(2,1)S(1)} %collective-permute-done.3.refs_4_.refs_8_), channel_id=1, source_target_pairs={{0,96},{16,112},{32,64},{48,80},{64,32},{80,48},{96,0},{112,16},{1... | collective-permute-start | bytes 1572872 | tf_op jit(solution)/shard_map/ppermute | solution.py:543
  52.1 6.6 %collective-permute-start.6 = (bf16[144,512]{1,0:T(8,128)(2,1)}, bf16[144,512]{1,0:T(8,128)(2,1)S(1)}, u32[]{:S(2)}, u32[]{:S(2)}) collective-permute-start(bf16[144,512]{1,0:T(8,128)(2,1)} %get-tuple-element.67), channel_id=1, source_target_pairs={{0,32},{16,48},{32,0},{48,16},{64,96},{80,112},{96,64},{112,80},{1... | collective-permute-start | bytes 442376 | tf_op jit(solution)/shard_map/ppermute | solution.py:543
  52.1 8.4 %collective-permute-start.7 = (bf16[144,512]{1,0:T(8,128)(2,1)}, bf16[144,512]{1,0:T(8,128)(2,1)}, u32[]{:S(2)}, u32[]{:S(2)}) collective-permute-start(bf16[144,512]{1,0:T(8,128)(2,1)} %get-tuple-element.68), channel_id=1, source_target_pairs={{0,16},{16,0},{32,48},{48,32},{64,80},{80,64},{96,112},{112,96},{1... | collective-permute-start | bytes 442376 | tf_op jit(solution)/shard_map/ppermute | solution.py:543
  54.7 7.9 %collective-permute-start.8 = (bf16[144,512]{1,0:T(8,128)(2,1)}, bf16[144,512]{1,0:T(8,128)(2,1)}, u32[]{:S(2)}, u32[]{:S(2)}) collective-permute-start(bf16[144,512]{1,0:T(8,128)(2,1)} %get-tuple-element.69), channel_id=1, source_target_pairs={{0,48},{16,32},{32,16},{48,0},{64,112},{80,96},{96,80},{112,64},{1... | collective-permute-start | bytes 442376 | tf_op jit(solution)/shard_map/ppermute | solution.py:543
  57.3 13.2 %collective-permute-start.13 = (bf16[256,1024]{1,0:T(8,128)(2,1)S(1)}, bf16[256,1024]{1,0:T(8,128)(2,1)S(1)}, u32[]{:S(2)}, u32[]{:S(2)}) collective-permute-start(bf16[256,1024]{1,0:T(8,128)(2,1)S(1)} %copy-done.2), channel_id=1, source_target_pairs={{0,1},{1,0},{2,3},{3,2},{4,5},{5,4},{6,7},{7,6},{8,9},{9,8},{10,11... | collective-permute-start | bytes 1572872 | tf_op jit(solution)/shard_map/ppermute | solution.py:555
  57.4 13.1 %collective-permute-start.14 = (bf16[256,1024]{1,0:T(8,128)(2,1)S(1)}, bf16[256,1024]{1,0:T(8,128)(2,1)S(1)}, u32[]{:S(2)}, u32[]{:S(2)}) collective-permute-start(bf16[256,1024]{1,0:T(8,128)(2,1)S(1)} %collective-permute-done.12.w2), channel_id=1, source_target_pairs={{0,1},{1,0},{2,3},{3,2},{4,5},{5,4},{6,7},{7,6},{8,9},{9,8},{10,11... | collective-permute-start | bytes 1572872 | tf_op jit(solution)/shard_map/ppermute | solution.py:555
  72.7 6.7 %collective-permute-start.16 = (bf16[32,1024]{1,0:T(8,128)(2,1)S(1)}, bf16[32,1024]{1,0:T(8,128)(2,1)S(1)}, u32[]{:S(2)}, u32[]{:S(2)}) collective-permute-start(bf16[32,1024]{1,0:T(8,128)(2,1)S(1)} %get-tuple-element.79), channel_id=1, source_target_pairs={{0,4},{1,5},{2,6},{3,7},{4,0},{5,1},{6,2},{7,3},{8,12},{9,13},{10,... | collective-permute-start | bytes 196616 | tf_op jit(solution)/shard_map/ppermute | solution.py:555
  75.6 5.5 %collective-permute-start.17 = (bf16[32,1024]{1,0:T(8,128)(2,1)S(1)}, bf16[32,1024]{1,0:T(8,128)(2,1)S(1)}, u32[]{:S(2)}, u32[]{:S(2)}) collective-permute-start(bf16[32,1024]{1,0:T(8,128)(2,1)S(1)} %get-tuple-element.80), channel_id=1, source_target_pairs={{0,6},{1,7},{2,4},{3,5},{4,2},{5,3},{6,0},{7,1},{8,14},{9,15},{10,... | collective-permute-start | bytes 196616 | tf_op jit(solution)/shard_map/ppermute | solution.py:555
  93.0 6.1 %collective-permute-start.20 = (bf16[32,1024]{1,0:T(8,128)(2,1)S(1)}, bf16[32,1024]{1,0:T(8,128)(2,1)S(1)}, u32[]{:S(2)}, u32[]{:S(2)}) collective-permute-start(bf16[32,1024]{1,0:T(8,128)(2,1)S(1)} %get-tuple-element.81.g0), channel_id=1, source_target_pairs={{0,6},{1,7},{2,4},{3,5},{4,2},{5,3},{6,0},{7,1},{8,14},{9,15},{10,... | collective-permute-start | bytes 196616 | tf_op jit(solution)/shard_map/ppermute | solution.py:555
  93.8 5.9 %collective-permute-start.19 = (bf16[32,1024]{1,0:T(8,128)(2,1)S(1)}, bf16[32,1024]{1,0:T(8,128)(2,1)S(1)}, u32[]{:S(2)}, u32[]{:S(2)}) collective-permute-start(bf16[32,1024]{1,0:T(8,128)(2,1)S(1)} %get-tuple-element.81.g0), channel_id=1, source_target_pairs={{0,4},{1,5},{2,6},{3,7},{4,0},{5,1},{6,2},{7,3},{8,12},{9,13},{10,... | collective-permute-start | bytes 196616 | tf_op jit(solution)/shard_map/ppermute | solution.py:555
  106.8 9.0 %collective-permute-start.26 = (bf16[144,512]{1,0:T(8,128)(2,1)S(1)}, bf16[144,512]{1,0:T(8,128)(2,1)S(1)}, u32[]{:S(2)}, u32[]{:S(2)}) collective-permute-start(bf16[144,512]{1,0:T(8,128)(2,1)S(1)} %get-tuple-element.89), channel_id=1, source_target_pairs={{0,48},{16,32},{32,16},{48,0},{64,112},{80,96},{96,80},{112,64},{1... | collective-permute-start | bytes 442376 | tf_op jit(solution)/shard_map/ppermute | solution.py:543
  109.8 8.8 %collective-permute-start.25 = (bf16[144,512]{1,0:T(8,128)(2,1)S(1)}, bf16[144,512]{1,0:T(8,128)(2,1)S(1)}, u32[]{:S(2)}, u32[]{:S(2)}) collective-permute-start(bf16[144,512]{1,0:T(8,128)(2,1)S(1)} %get-tuple-element.89), channel_id=1, source_target_pairs={{0,16},{16,0},{32,48},{48,32},{64,80},{80,64},{96,112},{112,96},{1... | collective-permute-start | bytes 442376 | tf_op jit(solution)/shard_map/ppermute | solution.py:543
  111.4 7.2 %collective-permute-start.24 = (bf16[144,512]{1,0:T(8,128)(2,1)S(1)}, bf16[144,512]{1,0:T(8,128)(2,1)S(1)}, u32[]{:S(2)}, u32[]{:S(2)}) collective-permute-start(bf16[144,512]{1,0:T(8,128)(2,1)S(1)} %get-tuple-element.88.refs_4_), channel_id=1, source_target_pairs={{0,32},{16,48},{32,0},{48,16},{64,96},{80,112},{96,64},{112,80},{1... | collective-permute-start | bytes 442376 | tf_op jit(solution)/shard_map/ppermute | solution.py:543
  137.2 34.6 %collective-permute-start.30 = (bf16[1024,256]{1,0:T(8,128)(2,1)S(1)}, bf16[1024,256]{1,0:T(8,128)(2,1)S(1)}, u32[]{:S(2)}, u32[]{:S(2)}) collective-permute-start(bf16[1024,256]{1,0:T(8,128)(2,1)S(1)} %get-tuple-element.100), channel_id=1, source_target_pairs={{0,96},{16,112},{32,64},{48,80},{64,32},{80,48},{96,0},{112,16},{1... | collective-permute-start | bytes 1572872 | tf_op jit(solution)/shard_map/ppermute | solution.py:543
  138.6 33.2 %collective-permute-start.31 = (bf16[1024,256]{1,0:T(8,128)(2,1)S(1)}, bf16[1024,256]{1,0:T(8,128)(2,1)S(1)}, u32[]{:S(2)}, u32[]{:S(2)}) collective-permute-start(bf16[1024,256]{1,0:T(8,128)(2,1)S(1)} %get-tuple-element.101), channel_id=1, source_target_pairs={{0,16},{16,0},{32,48},{48,32},{64,80},{80,64},{96,112},{112,96},{1... | collective-permute-start | bytes 1572872 | tf_op jit(solution)/shard_map/ppermute | solution.py:543
  140.1 31.7 %collective-permute-start.32 = (bf16[1024,256]{1,0:T(8,128)(2,1)S(1)}, bf16[1024,256]{1,0:T(8,128)(2,1)S(1)}, u32[]{:S(2)}, u32[]{:S(2)}) collective-permute-start(bf16[1024,256]{1,0:T(8,128)(2,1)S(1)} %get-tuple-element.102), channel_id=1, source_target_pairs={{0,112},{16,96},{32,80},{48,64},{64,48},{80,32},{96,16},{112,0},{1... | collective-permute-start | bytes 1572872 | tf_op jit(solution)/shard_map/ppermute | solution.py:543
  150.2 20.3 %collective-permute-start.28 = (bf16[128,512]{1,0:T(8,128)(2,1)S(1)}, bf16[128,512]{1,0:T(8,128)(2,1)S(1)}, u32[]{:S(2)}, u32[]{:S(2)}) collective-permute-start(bf16[128,512]{1,0:T(8,128)(2,1)S(1)} %get-tuple-element.95), channel_id=1, source_target_pairs={{0,16},{16,0},{32,48},{48,32},{64,80},{80,64},{96,112},{112,96},{1... | collective-permute-start | bytes 393224 | tf_op jit(solution)/shard_map/ppermute | solution.py:543
  154.8 15.7 %collective-permute-start.29 = (bf16[128,512]{1,0:T(8,128)(2,1)S(1)}, bf16[128,512]{1,0:T(8,128)(2,1)S(1)}, u32[]{:S(2)}, u32[]{:S(2)}) collective-permute-start(bf16[128,512]{1,0:T(8,128)(2,1)S(1)} %get-tuple-element.96), channel_id=1, source_target_pairs={{0,48},{16,32},{32,16},{48,0},{64,112},{80,96},{96,80},{112,64},{1... | collective-permute-start | bytes 393224 | tf_op jit(solution)/shard_map/ppermute | solution.py:543
  (34 other events, 373.2 us)
